TPU v7x, 256 devices: a whole 4x4x8 slice. The times are simulated.
256 devices in a mesh: leaf: 4 (over y), dom: 64 (over x, z, core).
Axes of the slice: x: 4, y: 4, z: 8, core: 2. Of those that a mesh axis runs over, the one named last changes fastest.
Arguments:
- parent_coords: float32 [3, 125, 8192], P(None, None, ('leaf', 'dom')), may hold values from -1.8 to 1.8
- coarse_coords: float32 [3, 125, 65536], P(None, None, ('leaf', 'dom')), may hold values from -1.8 to 1.8
- child_parent: int32 [65536], P(('leaf', 'dom')), may hold values from -1 to 31, as said below
- child_octant: int32 [65536], P(('leaf', 'dom')), may hold values from 0 to 7
- face_elem: int32 [65536], P(('leaf', 'dom')), may hold values from 0 to 255
- face_side: int32 [65536], P(('leaf', 'dom')), may hold values from 0 to 5
- face_owner: int32 [65536, 1], P(('leaf', 'dom')), may hold values from 0 to 255; in each aligned block of 256 rows (0 to 255, 256 to 511, ...) at most 2 rows name the same one
- coarse_elem: int32 [65536], P(('leaf', 'dom')), may hold values from 0 to 255
- coarse_side: int32 [65536], P(('leaf', 'dom')), may hold values from 0 to 5
- quadrant: int32 [65536], P(('leaf', 'dom')), may hold values from 0 to 3
Outputs:
- jac_det: float32 [125, 65536], P(None, ('leaf', 'dom'))
- face_normals: float32 [3, 25, 65536], P(None, None, ('leaf', 'dom'))
- coarse_partials: float32 [3, 150, 65536], P(None, None, ('leaf', 'dom'))
Inputs may be any that keep to these rules, and one draw needn't show every extreme that they name: `face_owner`: the rows of one device (aligned blocks of 256 records) name one owner at most 2 times; some owner is named exactly 2 times. `child_parent`: -1 names the last parent of the previous device block; the first device block has no -1; values never fall within a block.
All inputs are finite; a program needn't handle non-finite values.
Results may differ from a plain program's by a relative error of at most 0.0003.
Values sent between devices are 32-bit elements; how exact they have to be, the bound alone decides.
A program may use at most 128 MiB of HBM per device.

v0:
```python
import math

import jax
import jax.numpy as jnp
import numpy as np
from jax import lax
from jax.sharding import PartitionSpec as P


def passed_along(value, axis, steps):
    count = lax.axis_size(axis)
    first, last = (max(0, -steps), min(count, count - steps))
    return lax.ppermute(value, axis, [(source, source + steps) for source in range(first, last)])


def lobatto_nodes():
    return np.array([-1.0, -math.sqrt(3.0 / 7.0), 0.0, math.sqrt(3.0 / 7.0), 1.0])


def lagrange_table(targets):
    points = lobatto_nodes()
    table = np.ones((targets.shape[0], 5))
    for column in range(5):
        for others in range(5):
            if others != column:
                table[:, column] *= (targets - points[others]) / (points[column] - points[others])
    return table


def derivative_table():
    points = lobatto_nodes()
    table = np.zeros((5, 5))
    for target in range(5):
        for column in range(5):
            total = 0.0
            for others in range(5):
                if others != column:
                    term = 1.0 / (points[column] - points[others])
                    for remain in range(5):
                        if remain != column and remain != others:
                            term *= (points[target] - points[remain]) / (
                                points[column] - points[remain]
                            )
                    total += term
            table[target, column] = total
    return table


def lower_table():
    return lagrange_table((lobatto_nodes() - 1.0) / 2.0)


def upper_table():
    return lagrange_table((lobatto_nodes() + 1.0) / 2.0)


def apply_axis(table, field, axis):
    moved = jnp.tensordot(
        jnp.asarray(table, jnp.float32),
        field,
        axes=((1,), (axis,)),
        precision=lax.Precision.HIGHEST,
    )
    return jnp.moveaxis(moved, 0, axis)


def halves(field, axis, choose, lower, upper):
    return jnp.where(choose, apply_axis(upper, field, axis), apply_axis(lower, field, axis))


def build_children(parents, octant):
    field = parents
    lower, upper = (lower_table(), upper_table())
    for axis, weight in ((1, 4), (2, 2), (3, 1)):
        field = halves(field, axis, octant // weight % 2 == 1, lower, upper)
    return field


def jacobian_det(field):
    slope = derivative_table()
    grads = [apply_axis(slope, field, axis) for axis in (1, 2, 3)]
    first = grads[0][0] * (grads[1][1] * grads[2][2] - grads[2][1] * grads[1][2])
    second = grads[1][0] * (grads[0][1] * grads[2][2] - grads[2][1] * grads[0][2])
    third = grads[2][0] * (grads[0][1] * grads[1][2] - grads[1][1] * grads[0][2])
    return (first - second + third).reshape(125, -1)


def face_nodes(side):
    direction = side // 2
    level = side % 2 * 4
    fixed_stride = jnp.where(direction == 0, 25, jnp.where(direction == 1, 5, 1))
    first_stride = jnp.where(direction == 0, 5, 25)
    second_stride = jnp.where(direction == 2, 5, 1)
    places = jnp.arange(25, dtype=jnp.int32)[:, None]
    nodes = level * fixed_stride + places // 5 * first_stride + places % 5 * second_stride
    return nodes.astype(jnp.int32)


def face_values(field, elements, side):
    return field[:, face_nodes(side), elements[None, :]].reshape(3, 5, 5, -1)


def mortar(fine, coarse, quadrant):
    lower, upper, slope = (lower_table(), upper_table(), derivative_table())
    upper_first = quadrant // 2 == 1
    upper_second = quadrant % 2 == 1
    placed = halves(halves(coarse, 1, upper_first, lower, upper), 2, upper_second, lower, upper)
    merged = 0.5 * (fine + placed)
    along_first = apply_axis(slope, merged, 1)
    along_second = apply_axis(slope, merged, 2)
    normal = jnp.stack(
        [
            along_first[1] * along_second[2] - along_first[2] * along_second[1],
            along_first[2] * along_second[0] - along_first[0] * along_second[2],
            along_first[0] * along_second[1] - along_first[1] * along_second[0],
        ]
    )
    back = halves(normal, 2, upper_second, lower.T, upper.T)
    back = halves(back, 1, upper_first, lower.T, upper.T)
    return (normal, back)


def sum_partials(back_rows, valid, target_elem, target_side, coarse_count):
    masked = (back_rows * valid[None, :]).T
    element_key = (target_elem * 6 + target_side).astype(jnp.int32)
    total = jax.ops.segment_sum(masked, element_key, num_segments=coarse_count * 6)
    return total.reshape(coarse_count, 6, 3, 25).transpose(2, 1, 3, 0).reshape(3, 150, coarse_count)


def shards(
    parent_coords,
    coarse_coords,
    child_parent,
    child_octant,
    face_elem,
    face_side,
    face_owner,
    coarse_elem,
    coarse_side,
    quadrant,
):
    previous = passed_along(parent_coords[:, :, -1:], ("leaf", "dom"), 1)
    parent_pool = jnp.concatenate([previous, parent_coords], axis=2)
    elements_here = child_parent.shape[0]
    gathered = parent_pool[:, :, child_parent + 1].reshape(3, 5, 5, 5, elements_here)
    children = build_children(gathered, child_octant)
    flat_children = children.reshape(3, 125, elements_here)
    records = face_elem.shape[0]
    leaf_size = lax.axis_size("leaf")
    rank_total = leaf_size * lax.axis_size("dom")
    capacity = 2 * records // rank_total
    slot_total = 2 * records
    lane_count = slot_total // leaf_size
    owner = face_owner[:, 0]
    onehot = (owner[:, None] == jnp.arange(rank_total, dtype=jnp.int32)[None, :]).astype(jnp.int32)
    running = jnp.cumsum(onehot, axis=0)
    slot_rank = jnp.sum(running * onehot, axis=1) - 1
    position = owner * capacity + slot_rank
    coarse_count = coarse_coords.shape[2]
    fine_here = face_values(flat_children, face_elem, face_side)
    int_payload = jnp.stack([jnp.ones_like(coarse_elem), coarse_elem, coarse_side, quadrant])
    int_buffer = jnp.zeros((4, slot_total), jnp.int32).at[:, position].set(int_payload)
    buffer = (
        jnp.zeros((75, slot_total), jnp.float32).at[:, position].set(fine_here.reshape(75, records))
    )
    received, received_ints = (
        lax.all_to_all(
            lax.all_to_all(
                buffer.reshape(75, leaf_size, lane_count),
                "leaf",
                split_axis=1,
                concat_axis=1,
                tiled=True,
            ),
            "dom",
            split_axis=2,
            concat_axis=2,
            tiled=True,
        ),
        lax.all_to_all(
            lax.all_to_all(
                int_buffer.reshape(4, leaf_size, lane_count),
                "leaf",
                split_axis=1,
                concat_axis=1,
                tiled=True,
            ),
            "dom",
            split_axis=2,
            concat_axis=2,
            tiled=True,
        ),
    )
    jac_det = jacobian_det(children)
    received_ints = received_ints.reshape(4, slot_total)
    valid = received_ints[0].astype(jnp.float32)
    target_elem = received_ints[1]
    target_side = received_ints[2]
    fine = received.reshape(3, 5, 5, slot_total)
    coarse = face_values(coarse_coords, target_elem, target_side)
    normal, back = mortar(fine, coarse, received_ints[3])
    returned = lax.all_to_all(
        lax.all_to_all(
            normal.reshape(75, leaf_size, lane_count),
            "leaf",
            split_axis=1,
            concat_axis=1,
            tiled=True,
        ),
        "dom",
        split_axis=2,
        concat_axis=2,
        tiled=True,
    )
    face_normals = returned.reshape(75, slot_total)[:, position].reshape(3, 25, records)
    coarse_partials = sum_partials(
        back.reshape(75, slot_total), valid, target_elem, target_side, coarse_count
    )
    return (jac_det, face_normals, coarse_partials)


def solution(mesh):
    placed = (
        P(None, None, ("leaf", "dom")),
        P(None, None, ("leaf", "dom")),
        P(("leaf", "dom")),
        P(("leaf", "dom")),
        P(("leaf", "dom")),
        P(("leaf", "dom")),
        P(("leaf", "dom"), None),
        P(("leaf", "dom")),
        P(("leaf", "dom")),
        P(("leaf", "dom")),
    )
    return jax.shard_map(
        shards,
        mesh=mesh,
        in_specs=placed,
        out_specs=(
            P(None, ("leaf", "dom")),
            P(None, None, ("leaf", "dom")),
            P(None, None, ("leaf", "dom")),
        ),
        check_vma=False,
    )
```

profile of v0, /device:TPU:1, one launch (start us, length us, event | category | flops | bytes accessed | tf_op | source)
XLA Modules:
  0.0 572.2 jit_solution(2913315883657598925)
XLA Ops:
  4.2 1.2 scatter_custom_fusion.1
  6.2 5.0 all-to-all-start.2
  12.0 4.4 collective-permute-start
  18.7 9.4 %copy.264 = f32[3,125,256]{0,2,1:T(8,128)} copy(f32[3,125,256]{2,1,0:T(8,128)} %param.30) | data formatting | bytes 768000 | tf_op args[1]
  28.2 1.0 gather_fusion
  37.5 10.9 %all-to-all-start.3 = ((s32[4,4,128]{1,0,2:T(4,128)}), s32[4,4,128]{1,0,2:T(4,128)}, u32[]{:S(2)}, u32[]{:S(2)}) async-start(s32[4,4,128]{1,0,2:T(4,128)} %copy.260), calls=%async_computation.3 | async-start | bytes 524288 | tf_op jit(solution)/shard_map/all_to_all | solution.py:180
  48.6 10.0 %copy.293 = f32[3,5,5,5,256]{0,4,3,2,1:T(8,128)} copy(f32[3,5,5,5,256]{4,3,2,1,0:T(8,128)S(1)} %fusion) | data formatting | bytes 768000 | tf_op jit(solution)/shard_map/reshape | solution.py:147
  58.5 45.6 %gather_fusion.1 = f32[6400,3]{1,0:T(8,128)S(1)} fusion(f32[3,125,256]{0,2,1:T(8,128)} %bitcast.168, s32[6400]{0:T(1024)S(1)} %reshape.523), kind=kCustom, calls=%fused_computation.1 | custom fusion | bytes 204800 | tf_op jit(solution)/shard_map/gather | solution.py:100
  104.2 2.1 copy.253
  107.3 1.2 scatter_custom_fusion
  110.1 4.4 all-to-all-start
  114.5 1.6 fusion.72
  116.5 391.6 %gather_fusion.2 = f32[12800,3]{1,0:T(8,128)} fusion(f32[3,125,256]{0,2,1:T(8,128)} %copy.264, s32[12800]{0:T(1024)S(1)} %reshape.529), kind=kCustom, calls=%fused_computation.2 | custom fusion | bytes 409600 | tf_op jit(solution)/shard_map/gather | solution.py:100
  508.1 4.6 copy.265
  514.5 12.9 %all-to-all-start.1 = ((f32[75,4,128]{0,1,2:T(4,128)}), f32[75,4,128]{0,1,2:T(4,128)S(1)}, u32[]{:S(2)}, u32[]{:S(2)}) async-start(f32[75,4,128]{0,1,2:T(4,128)} %copy.256), calls=%async_computation.1 | async-start | bytes 524288 | tf_op jit(solution)/shard_map/all_to_all | solution.py:167
  527.9 11.6 %all-to-all-done.1 = f32[75,4,128]{0,1,2:T(4,128)S(1)} async-done(((f32[75,4,128]{0,1,2:T(4,128)}), f32[75,4,128]{0,1,2:T(4,128)S(1)}, u32[]{:S(2)}, u32[]{:S(2)}) %all-to-all-start.1) | async-done | bytes 153632 | tf_op jit(solution)/shard_map/all_to_all | solution.py:167
  542.4 3.3 all-to-all-start.4
  546.6 4.1 all-to-all-done.4
  551.6 7.2 %all-to-all-start.5 = ((f32[75,4,128]{0,1,2:T(4,128)}), f32[75,4,128]{0,1,2:T(4,128)S(1)}, u32[]{:S(2)}, u32[]{:S(2)}) async-start(f32[75,4,128]{0,1,2:T(4,128)} %copy.274), calls=%async_computation.5 | async-start | bytes 524288 | tf_op jit(solution)/shard_map/all_to_all | solution.py:202
  559.5 3.5 scatter_custom_fusion.2
  563.0 2.9 reshape.512
  565.8 2.1 copy.284
  567.9 1.9 reshape.513
  569.8 0.9 all-to-all-done.5
  (106 shorter events, 27.5 us)
Async XLA Ops:
  6.2 30.5 %all-to-all-start.2 = ((s32[4,4,128]{2,0,1:T(4,128)}), s32[4,4,128]{2,0,1:T(4,128)S(1)}, u32[]{:S(2)}, u32[]{:S(2)}) async-start(s32[4,4,128]{2,0,1:T(4,128)} %copy.259), calls=%async_computation.2 | async-start | bytes 16384 | tf_op jit(solution)/shard_map/all_to_all | solution.py:181
  12.0 16.1 %collective-permute-start = (f32[3,125,1]{1,0,2:T(4,128)S(1)}, f32[3,125,1]{1,0,2:T(4,128)S(1)}, u32[]{:S(2)}, u32[]{:S(2)}) collective-permute-start(f32[3,125,1]{1,0,2:T(4,128)S(1)} %slice.115), channel_id=1, source_target_pairs={{0,1},{1,2},{2,3},{3,4},{4,5},{5,6},{6,7},{7,8},{8,9},{9,10},{10,1... | collective-permute-start | bytes 4508 | tf_op jit(solution)/shard_map/ppermute | solution.py:13
  18.7 10.8 %copy-start.2 = (f32[5,5,1,1,1]{1,0,4,3,2:T(8,128)S(1)}, f32[5,5,1,1,1]{1,0,4,3,2:T(8,128)}, u32[]{:S(2)}) copy-start(f32[5,5,1,1,1]{1,0,4,3,2:T(8,128)} %constant.201) | copy-start | bytes 304
  18.7 11.6 %copy-start.1 = (f32[5,5,1,1,1]{1,0,4,3,2:T(8,128)S(1)}, f32[5,5,1,1,1]{1,0,4,3,2:T(8,128)}, u32[]{:S(2)}) copy-start(f32[5,5,1,1,1]{1,0,4,3,2:T(8,128)} %constant.202) | copy-start | bytes 304
  28.1 6.0 %copy-start = (f32[5,5,1,1,1]{1,0,4,3,2:T(8,128)S(1)}, f32[5,5,1,1,1]{1,0,4,3,2:T(8,128)}, u32[]{:S(2)}) copy-start(f32[5,5,1,1,1]{1,0,4,3,2:T(8,128)} %constant.203) | copy-start | bytes 304
  37.5 72.6 %all-to-all-start.3 = ((s32[4,4,128]{1,0,2:T(4,128)}), s32[4,4,128]{1,0,2:T(4,128)}, u32[]{:S(2)}, u32[]{:S(2)}) async-start(s32[4,4,128]{1,0,2:T(4,128)} %copy.260), calls=%async_computation.3 | async-start | bytes 524288 | tf_op jit(solution)/shard_map/all_to_all | solution.py:180
  110.1 403.6 %all-to-all-start = ((f32[75,4,128]{2,0,1:T(8,128)}), f32[75,4,128]{2,0,1:T(8,128)S(1)}, u32[]{:S(2)}, u32[]{:S(2)}) async-start(f32[75,4,128]{2,0,1:T(8,128)} %copy.255), calls=%async_computation | async-start | bytes 327680 | tf_op jit(solution)/shard_map/all_to_all | solution.py:168
  116.5 396.4 %copy-start.7 = (f32[5,5,1,1]{1,0,3,2:T(8,128)S(1)}, f32[5,5,1,1]{1,0,3,2:T(8,128)}, u32[]{:S(2)}) copy-start(f32[5,5,1,1]{1,0,3,2:T(8,128)} %constant.204) | copy-start | bytes 304
  116.5 396.8 %copy-start.6 = (f32[5,5,1,1]{1,0,3,2:T(8,128)S(1)}, f32[5,5,1,1]{1,0,3,2:T(8,128)}, u32[]{:S(2)}) copy-start(f32[5,5,1,1]{1,0,3,2:T(8,128)} %constant.205) | copy-start | bytes 304
  508.1 32.0 %copy-start.5 = (f32[5,5,1,1]{1,0,3,2:T(8,128)S(1)}, f32[5,5,1,1]{1,0,3,2:T(8,128)}, u32[]{:S(2)}) copy-start(f32[5,5,1,1]{1,0,3,2:T(8,128)} %constant.206) | copy-start | bytes 304
  508.1 33.1 %copy-start.4 = (f32[5,5,1,1]{1,0,3,2:T(8,128)S(1)}, f32[5,5,1,1]{1,0,3,2:T(8,128)}, u32[]{:S(2)}) copy-start(f32[5,5,1,1]{1,0,3,2:T(8,128)} %constant.207) | copy-start | bytes 304
  508.1 37.6 %copy-start.3 = (f32[5,5,1,1]{1,0,3,2:T(8,128)S(1)}, f32[5,5,1,1]{1,0,3,2:T(8,128)}, u32[]{:S(2)}) copy-start(f32[5,5,1,1]{1,0,3,2:T(8,128)} %constant.208) | copy-start | bytes 304
  514.5 24.9 %all-to-all-start.1 = ((f32[75,4,128]{0,1,2:T(4,128)}), f32[75,4,128]{0,1,2:T(4,128)S(1)}, u32[]{:S(2)}, u32[]{:S(2)}) async-start(f32[75,4,128]{0,1,2:T(4,128)} %copy.256), calls=%async_computation.1 | async-start | bytes 524288 | tf_op jit(solution)/shard_map/all_to_all | solution.py:167
  542.4 8.3 %all-to-all-start.4 = ((f32[75,4,128]{2,0,1:T(8,128)}), f32[75,4,128]{2,0,1:T(8,128)S(1)}, u32[]{:S(2)}, u32[]{:S(2)}) async-start(f32[75,4,128]{2,0,1:T(8,128)} %copy.273), calls=%async_computation.4 | async-start | bytes 327680 | tf_op jit(solution)/shard_map/all_to_all | solution.py:203
  551.6 19.2 %all-to-all-start.5 = ((f32[75,4,128]{0,1,2:T(4,128)}), f32[75,4,128]{0,1,2:T(4,128)S(1)}, u32[]{:S(2)}, u32[]{:S(2)}) async-start(f32[75,4,128]{0,1,2:T(4,128)} %copy.274), calls=%async_computation.5 | async-start | bytes 524288 | tf_op jit(solution)/shard_map/all_to_all | solution.py:202
where the time goes:
time: 576 us; the launch traced here: 572 us
  local copies, waits for them, and re-layouts  487 us (85%)
  starting transfers between devices  48.1 us (8%)
  waiting for transfers between devices  16.6 us (3%)
  matrix products  10.9 us (2%)
  other arithmetic  8.77 us (2%)
    gather x4, local copies, waits for them, and re-layouts, face_values(): return field[:, face_nodes(side), elements[None, :]].reshape(3, 5, 5, -1)  444 us
    all_to_all x1, starting transfers between devices, shards(): lax.all_to_all(lax.all_to_all(buffer.reshape(75, leaf_size, lane_count),...  12.9 us
    all_to_all x1, waiting for transfers between devices, shards(): lax.all_to_all(lax.all_to_all(buffer.reshape(75, leaf_size, lane_count),...  11.6 us
  transfers between devices with their start and end apart: 7, of which 3 were waited for; matrix products, arithmetic and copies ran while one was open for 86% of the time, Pallas kernels for 0%

commit v1 on v0

v1 whole, which is shorter than its diff:
```python
import functools
import math

import jax
import jax.numpy as jnp
import ml_dtypes
import numpy as np
from jax import lax
from jax.experimental import pallas as pl
from jax.experimental.pallas import tpu as pltpu
from jax.sharding import PartitionSpec as P

F32 = jnp.float32
BF16 = jnp.bfloat16
POOL = 40
MIDDLE = 62
VALID, ELEM, SIDE, QUAD, FSIDE, PROW, OCT = 75, 76, 77, 78, 80, 81, 82


def lobatto_nodes():
    return np.array([-1.0, -math.sqrt(3.0 / 7.0), 0.0, math.sqrt(3.0 / 7.0), 1.0])


def lagrange_table(targets):
    points = lobatto_nodes()
    table = np.ones((targets.shape[0], 5))
    for column in range(5):
        for others in range(5):
            if others != column:
                table[:, column] *= (targets - points[others]) / (points[column] - points[others])
    return table


def derivative_table():
    points = lobatto_nodes()
    table = np.zeros((5, 5))
    for target in range(5):
        for column in range(5):
            total = 0.0
            for others in range(5):
                if others != column:
                    term = 1.0 / (points[column] - points[others])
                    for remain in range(5):
                        if remain != column and remain != others:
                            term *= (points[target] - points[remain]) / (
                                points[column] - points[remain]
                            )
                    total += term
            table[target, column] = total
    return table


def f32_table(table):
    return table.astype(np.float32).astype(np.float64)


LOWER = f32_table(lagrange_table((lobatto_nodes() - 1.0) / 2.0))
UPPER = f32_table(lagrange_table((lobatto_nodes() + 1.0) / 2.0))
SLOPE = f32_table(derivative_table())
EYE = np.eye(5)


def halves_of(table):
    high = table.astype(np.float32).astype(ml_dtypes.bfloat16)
    low = (table - high.astype(np.float64)).astype(np.float32).astype(ml_dtypes.bfloat16)
    return high, low


def side_nodes(side):
    direction, level = side // 2, side % 2 * 4
    fixed = (25, 5, 1)[direction]
    first = 5 if direction == 0 else 25
    second = 5 if direction == 2 else 1
    return [level * fixed + a * first + b * second for a in range(5) for b in range(5)]


def child_constant():
    table = np.zeros((128, 8 * 128))
    for octant in range(8):
        picks = [UPPER if octant & bit else LOWER for bit in (4, 2, 1)]
        whole = np.kron(np.kron(picks[0], picks[1]), picks[2])
        table[:125, octant * 128 : octant * 128 + 125] = whole.T
    return np.concatenate(halves_of(table), axis=0)


def slope_constant():
    table = np.zeros((384, 128))
    for direction in range(3):
        picks = [SLOPE if axis == direction else EYE for axis in range(3)]
        whole = np.kron(np.kron(picks[0], picks[1]), picks[2])
        table[direction * 128 : direction * 128 + 125, :125] = whole
    return np.concatenate(halves_of(table), axis=1)


def side_constant():
    rows = np.full((1, 768), -1.0, np.float32)
    for side in range(6):
        for coord in range(3):
            at = side * 128 + coord * 25
            rows[0, at : at + 25] = [coord * 128 + node for node in side_nodes(side)]
    return rows


def quadrant_tables():
    for quadrant in range(4):
        first = UPPER if quadrant & 2 else LOWER
        second = UPPER if quadrant & 1 else LOWER
        yield np.kron(first, second)


def tangent_constant():
    slopes = [np.kron(SLOPE, EYE), np.kron(EYE, SLOPE)]
    parts = []
    for placed in [np.eye(25)] + list(quadrant_tables()):
        table = np.zeros((128, 256))
        for which, slope in enumerate(slopes):
            whole = 0.5 * (slope @ placed)
            for spot, coord in enumerate((0, 1, 2, 0, 1)):
                at = which * 128 + spot * 25
                table[coord * 25 : coord * 25 + 25, at : at + 25] = whole.T
        parts += halves_of(table)
    return np.concatenate(parts, axis=0)


def back_constant():
    parts = []
    for placed in quadrant_tables():
        table = np.zeros((128, 128))
        for coord in range(3):
            at = coord * 25
            table[at : at + 25, at : at + 25] = placed
        parts += halves_of(table)
    return np.concatenate(parts, axis=0)


def dot(left, right):
    return lax.dot_general(left, right, (((1,), (0,)), ((), ())), preferred_element_type=F32)


def dot_nt(left, right):
    return lax.dot_general(left, right, (((1,), (1,)), ((), ())), preferred_element_type=F32)


def split(value):
    high = value.astype(BF16)
    return high, (value - high.astype(F32)).astype(BF16)


def triple(value, axis=1):
    high, low = split(value)
    return jnp.concatenate([high, low, high], axis=axis)


def tripled(constant, size, axis=0):
    parts = []
    for at in range(0, constant.shape[axis], 2 * size):
        high = lax.slice_in_dim(constant, at, at + size, axis=axis)
        low = lax.slice_in_dim(constant, at + size, at + 2 * size, axis=axis)
        parts += [high, high, low]
    return jnp.concatenate(parts, axis=axis)


def side_matrix(rows):
    return ones_where(iota((384, rows.shape[1]), 0) == rows)


def iota(shape, axis):
    return lax.broadcasted_iota(jnp.int32, shape, axis).astype(F32)


def ones_where(condition):
    return jnp.where(condition, 1.0, 0.0).astype(BF16)


def pick(blocks, key):
    chosen = blocks[0]
    for number in range(1, len(blocks)):
        chosen = jnp.where(key == float(number), blocks[number], chosen)
    return chosen


def lane_blocks(value, count):
    return [value[:, 128 * b : 128 * b + 128] for b in range(count)]


def positions(owner):
    records = owner.shape[1]
    column = columns_of(owner)[:, 0:1]
    same = (column == owner) & (iota((records, records), 0) < iota((records, records), 1))
    return owner * 2.0 + jnp.sum(jnp.where(same, 1.0, 0.0), axis=0, keepdims=True)


def columns_of(rows):
    count = rows.shape[1]
    eye = ones_where(iota((count, count), 0) == iota((count, count), 1))
    padded = jnp.broadcast_to(rows, (8, count)) if rows.shape[0] == 1 else rows
    return dot_nt(eye, padded.astype(BF16))


def child_table(pool, child_k):
    table = dot(triple(pool), tripled(child_k, 128))
    stacked = [
        jnp.concatenate(
            [
                table[c * POOL : (c + 1) * POOL, o * 128 : o * 128 + 128]
                for c in range(3)
            ],
            axis=1,
        )
        for o in range(8)
    ]
    high, low = split(jnp.concatenate(stacked, axis=0))
    return jnp.concatenate([high, low], axis=0)


def row_picker(key, size):
    hot = ones_where(key == iota((key.shape[0], size), 1))
    return jnp.concatenate([hot, hot], axis=1)


def messages(table, side_k, slots, position, ints):
    faces = dot(table, side_k).astype(BF16)
    hot = ones_where(iota((slots, position.shape[1]), 0) == position)
    carried = dot_nt(hot, ints.astype(BF16))
    filled = carried[:, VALID : VALID + 1]
    key = carried[:, OCT : OCT + 1] * float(POOL) + carried[:, PROW : PROW + 1]
    picker = row_picker(jnp.where(filled > 0.5, key, -1.0), 8 * POOL)
    sides = dot(picker, faces)
    face = pick(lane_blocks(sides, 6), carried[:, FSIDE : FSIDE + 1])
    return jnp.where(iota(face.shape, 1) < 75.0, face, carried)


def determinants(table, slope_k, keys):
    children = dot(row_picker(keys, 8 * POOL), table)
    slope_k = tripled(slope_k, 128, 1)
    grads = [dot_nt(slope_k, triple(block)) for block in lane_blocks(children, 3)]
    g = [[grads[c][128 * d : 128 * d + 128] for c in range(3)] for d in range(3)]
    first = g[0][0] * (g[1][1] * g[2][2] - g[2][1] * g[1][2])
    second = g[1][0] * (g[0][1] * g[2][2] - g[2][1] * g[0][2])
    third = g[2][0] * (g[0][1] * g[1][2] - g[1][1] * g[0][2])
    return first - second + third


def coarse_faces(coarse, side_k):
    high, low = split(coarse.T)
    return jnp.concatenate([dot(high, side_k), dot(low, side_k)], axis=1).astype(BF16)


def mortar(message, faces, tangent_k):
    slots = message.shape[0]
    elements = faces.shape[0]
    filled = message[:, VALID : VALID + 1] > 0.5
    elem = jnp.where(filled, message[:, ELEM : ELEM + 1], -1.0)
    side, quad = message[:, SIDE : SIDE + 1], message[:, QUAD : QUAD + 1]
    hot = ones_where(elem == iota((slots, elements), 1))
    blocks = lane_blocks(dot(hot, faces), 12)
    high, low = pick(blocks[:6], side), pick(blocks[6:], side)
    parts = [triple(message)]
    for number in range(4):
        mine = quad == float(number)
        this_high = jnp.where(mine, high, 0.0).astype(BF16)
        this_low = jnp.where(mine, low, 0.0).astype(BF16)
        parts += [this_high, this_low, this_high]
    tangents = dot(jnp.concatenate(parts, axis=1), tripled(tangent_k, 128))
    t1, t2 = tangents[:, :128], tangents[:, 128:]
    ahead = lambda value, count: pltpu.roll(value, 128 - 25 * count, 1)
    return ahead(t1, 1) * ahead(t2, 2) - ahead(t1, 2) * ahead(t2, 1)


def partial_sums(normal, message, back_k, elements):
    slots = message.shape[0]
    filled = message[:, VALID : VALID + 1] > 0.5
    side, quad = message[:, SIDE : SIDE + 1], message[:, QUAD : QUAD + 1]
    key = side * float(elements) + message[:, ELEM : ELEM + 1]
    key = jnp.where(filled, key, -1.0)
    parts = []
    for number in range(4):
        parts.append(triple(jnp.where(quad == float(number), normal, 0.0)))
    back = dot(jnp.concatenate(parts, axis=1), tripled(back_k, 128))
    high, low = split(back.T)
    hot = ones_where(key == iota((slots, 6 * elements), 1))
    both = dot(jnp.concatenate([high, low], axis=0), hot)
    return both[:128] + both[128:]


def face_rows(returned, position):
    hot = ones_where(iota((returned.shape[0], position.shape[1]), 0) == position)
    high, low = split(returned.T)
    both = dot(jnp.concatenate([high, low], axis=0), hot)
    return both[:128] + both[128:]


def fill_pool(pool, parents, previous):
    pool[...] = jnp.zeros(pool.shape, F32)
    for c in range(3):
        own = parents[c]
        pool[c * POOL : c * POOL + 32, 0:125] = own - own[:, MIDDLE : MIDDLE + 1]
        last = previous[c : c + 1, 0:125]
        pool[c * POOL + 32 : c * POOL + 33, 0:125] = last - last[:, MIDDLE : MIDDLE + 1]


def fill_coarse(scratch, coarse):
    for c in range(3):
        scratch[c * 128 + 120 : c * 128 + 128, :] = jnp.zeros((8, coarse.shape[2]), F32)
        whole = coarse[c]
        scratch[c * 128 : c * 128 + 125, :] = whole - whole[MIDDLE : MIDDLE + 1]


def fill_ints(scratch, parent, octant, elem, side, c_elem, c_side, quad):
    scratch[...] = jnp.zeros(scratch.shape, F32)
    elements = parent.shape[1]
    parent = jnp.where(parent < 0.0, 32.0, parent)
    both = jnp.concatenate([parent, octant, jnp.zeros((6, elements), F32)], axis=0)
    hot = ones_where(iota((elements, elem.shape[1]), 0) == elem)
    chosen = dot(both.astype(BF16), hot)
    scratch[VALID : VALID + 1, :] = jnp.ones_like(elem)
    scratch[ELEM : ELEM + 1, :] = c_elem
    scratch[SIDE : SIDE + 1, :] = c_side
    scratch[QUAD : QUAD + 1, :] = quad
    scratch[FSIDE : FSIDE + 1, :] = side
    scratch[PROW : PROW + 1, :] = chosen[0:1]
    scratch[OCT : OCT + 1, :] = chosen[1:2]
    turned = columns_of(both)
    return turned[:, 1:2] * float(POOL) + turned[:, 0:1]


def fine_kernel(slots, parents, previous, parent, octant, elem, side, owner, c_elem, c_side, quad,
                child_k, side_k, slope_k, message_out, jac_out, pool, ints):
    rows = [r[...].astype(F32) for r in (parent, octant, elem, side, c_elem, c_side, quad)]
    fill_pool(pool, parents, previous)
    keys = fill_ints(ints, *rows)
    table = child_table(pool[...], child_k[...])
    position = positions(owner[...].astype(F32))
    message_out[...] = messages(table, side_matrix(side_k[...]), slots, position, ints[...])
    jac_out[...] = determinants(table, slope_k[...], keys)[0:125]


def mortar_kernel(message_in, coarse, side_k, tangent_k, back_k, normal_out, partial_out, scratch):
    elements = coarse.shape[2]
    fill_coarse(scratch, coarse)
    faces = coarse_faces(scratch[...], side_matrix(side_k[...]))
    message = message_in[...]
    normal = mortar(message, faces, tangent_k[...])
    normal_out[...] = normal
    sums = partial_sums(normal, message, back_k[...], elements)
    write_partials(partial_out, sums, elements)


def write_partials(partial_out, sums, elements):
    for c in range(3):
        for s in range(6):
            partial_out[c, s * 25 : s * 25 + 25, :] = sums[
                c * 25 : c * 25 + 25, s * elements : (s + 1) * elements
            ]


def final_kernel(returned, owner, normals_out):
    rows = face_rows(returned[...], positions(owner[...].astype(F32)))
    for c in range(3):
        normals_out[c] = rows[c * 25 : c * 25 + 25]


def call(kernel, shapes, scratch, *args):
    return pl.pallas_call(
        kernel,
        out_shape=shapes,
        scratch_shapes=scratch,
        compiler_params=pltpu.CompilerParams(vmem_limit_bytes=48 << 20),
    )(*args)


def shards(parents, coarse, parent, octant, elem, side, owner, c_elem, c_side, quad):
    axes = ("leaf", "dom")
    ranks = lax.axis_size(axes)
    slots = 2 * ranks
    records, elements = elem.shape[0], parent.shape[0]
    row = lambda value: value.reshape(1, -1)
    previous = lax.ppermute(
        parents[:, :, -1], axes, [(source, source + 1) for source in range(ranks - 1)]
    )
    side_k = side_constant()
    message, jac = call(
        functools.partial(fine_kernel, slots),
        (
            jax.ShapeDtypeStruct((slots, 128), F32),
            jax.ShapeDtypeStruct((125, elements), F32),
        ),
        [pltpu.VMEM((3 * POOL, 128), F32), pltpu.VMEM((128, records), F32)],
        parents.transpose(0, 2, 1), previous, row(parent), row(octant), row(elem), row(side),
        row(owner), row(c_elem), row(c_side), row(quad),
        jnp.asarray(child_constant()), jnp.asarray(side_k), jnp.asarray(slope_constant()),
    )
    arrived = lax.all_to_all(message.reshape(ranks, 2, 128), axes, 0, 0, tiled=True)
    normal, partials = call(
        mortar_kernel,
        (
            jax.ShapeDtypeStruct((slots, 128), F32),
            jax.ShapeDtypeStruct((3, 150, coarse.shape[2]), F32),
        ),
        [pltpu.VMEM((384, coarse.shape[2]), F32)],
        arrived.reshape(slots, 128), coarse,
        jnp.asarray(side_k), jnp.asarray(tangent_constant()),
        jnp.asarray(back_constant()),
    )
    returned = lax.all_to_all(normal.reshape(ranks, 2, 128), axes, 0, 0, tiled=True)
    normals = call(
        final_kernel,
        jax.ShapeDtypeStruct((3, 25, records), F32),
        [],
        returned.reshape(slots, 128), row(owner),
    )
    return jac, normals, partials


def solution(mesh):
    whole = P(None, None, ("leaf", "dom"))
    line = P(("leaf", "dom"))
    return jax.shard_map(
        shards,
        mesh=mesh,
        in_specs=(whole, whole, line, line, line, line, P(("leaf", "dom"), None), line, line, line),
        out_specs=(P(None, ("leaf", "dom")), whole, whole),
        check_vma=False,
    )
```

time: 576 us -> 72.8 us (0.13)
  local copies, waits for them, and re-layouts: 487 us -> 4.26 us
  blocking collectives: 0 us -> 53.1 us
  starting transfers between devices: 48.1 us -> 4.92 us
  waiting for transfers between devices: 16.6 us -> 0.71 us
  matrix products: 10.9 us -> 0 us
  Pallas kernels: 0 us -> 8.8 us
  other arithmetic: 8.77 us -> 0 us
    gather x8 -> x0, local copies, waits for them, and re-layouts: 446 us -> none  [the longest x4 444 us: face_values(): return field[:, face_nodes(side), elements[None, :]].reshape(3, 5, 5, -1)]
    all_to_all x0 -> x2, blocking collectives: none -> 53.1 us  [the longest x1 31.8 us: shards(): lax.all_to_all(message.reshape(ranks, 2, 128), axes, 0, 0, tiled=True)]
    all_to_all x6 -> x0, starting transfers between devices: 43.7 us -> none  [the longest x1 12.9 us: shards(): lax.all_to_all(lax.all_to_all(buffer.reshape(75, leaf_size, lane_count),...]
    reshape x11 -> x0, local copies, waits for them, and re-layouts: 17.8 us -> none  [the longest x1 9.95 us: shards(): flat_children = children.reshape(3, 125, elements_here)]
    all_to_all x6 -> x0, waiting for transfers between devices: 16.6 us -> none  [the longest x1 11.6 us: shards(): lax.all_to_all(lax.all_to_all(buffer.reshape(75, leaf_size, lane_count),...]
    dot_general x19 -> x0, matrix products: 10.9 us -> none  [apply_axis(): jnp.tensordot(jnp.asarray(table, jnp.float32), field, axes=((1,), (axis,)...]
    pallas_call x0 -> x3, Pallas kernels: none -> 8.8 us  [call(): pl.pallas_call(kernel, out_shape=shapes, scratch_shapes=scratch, compiler...]
    unnamed x22 -> x31, local copies, waits for them, and re-layouts: 10.5 us -> 3.54 us
  transfers between devices with their start and end apart: 7 -> 1, of which waited for: 3 -> 1; matrix products, arithmetic and copies ran while one was open for 86% -> 0% of each run, Pallas kernels for 0% -> 0%
where the time goes in v1:
time: 72.8 us; the launch traced here: 72.5 us
  blocking collectives  53.1 us (73%)
  Pallas kernels  8.8 us (12%)
  starting transfers between devices  4.92 us (7%)
  local copies, waits for them, and re-layouts  4.26 us (6%)
    all_to_all x1, blocking collectives, shards(): lax.all_to_all(message.reshape(ranks, 2, 128), axes, 0, 0, tiled=True)  31.8 us
    all_to_all x1, blocking collectives, shards(): lax.all_to_all(normal.reshape(ranks, 2, 128), axes, 0, 0, tiled=True)  21.2 us
    pallas_call x3, Pallas kernels, call(): pl.pallas_call(kernel, out_shape=shapes, scratch_shapes=scratch, compiler...  8.8 us
    ppermute x1, starting transfers between devices, shards(): lax.ppermute(parents[:, :, -1], axes, [(source, source + 1) for source in...  4.92 us
    unnamed x31, local copies, waits for them, and re-layouts  3.54 us
  transfers between devices with their start and end apart: 1, of which 1 were waited for; matrix products, arithmetic and copies ran while one was open for 0% of the time, Pallas kernels for 0%

profile of v1, /device:TPU:1, one launch (start us, length us, event | category | flops | bytes accessed | tf_op | source)
XLA Modules:
  0.0 72.5 jit_solution(5476953235205890301)
XLA Ops:
  0.6 0.7 slice.3
  1.3 4.9 %collective-permute-start = (f32[3,125]{1,0:T(4,128)S(1)}, f32[3,125]{1,0:T(4,128)S(1)}, u32[]{:S(2)}, u32[]{:S(2)}) collective-permute-start(f32[3,125]{1,0:T(4,128)S(1)} %bitcast.30), channel_id=1, source_target_pairs={{0,1},{1,2},{2,3},{3,4},{4,5},{5,6},{6,7},{7,8},{8,9},{9,10},{10,1... | collective-permute-start | bytes 4508 | tf_op jit(solution)/shard_map/ppermute | solution.py:378
  6.3 0.7 collective-permute-done.previous
  7.0 0.0 copy-start.10
  7.0 0.0 copy-start.6
  7.0 0.0 copy-start.8
  7.0 0.0 copy-start.7
  7.1 0.6 copy-done.13
  7.7 0.0 copy-done.14
  7.7 0.0 copy-done.11
  7.7 0.0 copy-done.12
  7.7 0.0 copy-done.9
  7.7 0.0 copy-done.10
  7.8 0.0 copy-done.6
  7.8 0.0 copy-done.8
  7.8 0.0 copy-done.7
  7.8 1.0 %copy-done.1 = bf16[256,1024]{1,0:T(8,128)(2,1)S(1)} copy-done((bf16[256,1024]{1,0:T(8,128)(2,1)S(1)}, bf16[256,1024]{1,0:T(8,128)(2,1)}, u32[]{:S(2)}) %copy-start.1) | copy-done | bytes 524312
  8.8 0.9 %copy-done.4 = bf16[384,256]{1,0:T(8,128)(2,1)S(1)} copy-done((bf16[384,256]{1,0:T(8,128)(2,1)S(1)}, bf16[384,256]{1,0:T(8,128)(2,1)}, u32[]{:S(2)}) %copy-start.4) | copy-done | bytes 196632
  9.8 0.8 %copy-done.5 = f32[3,125,32]{1,2,0:T(8,128)S(1)} copy-done((f32[3,125,32]{1,2,0:T(8,128)S(1)}, f32[3,125,32]{1,2,0:T(8,128)}, u32[]{:S(2)}) %copy-start.5) | copy-done | bytes 48024
  10.6 3.0 %shard_map.166 = (f32[512,128]{1,0:T(8,128)S(1)}, f32[125,256]{1,0:T(8,128)}) custom-call(f32[3,32,125]{2,1,0:T(8,128)S(1)} %bitcast.20, f32[3,125]{1,0:T(4,128)S(1)} %collective-permute-done.previous, s32[1,256]{1,0:T(1,128)S(1)} %bitcast.23, s32[1,256]{1,0:T(1,128)S(1)} %bitcast.24, s32[1,256]{1,0:T(1,128)S(1)} %bitcast.25, s32[1,256]{1,0:T(1,128)S(1)} %bitcast.26, ...), custom_call_target="tpu_custom_call" | custom-call | tf_op jit(solution)/shard_map/pallas_call | solution.py:364
  13.6 31.8 %all_to_all.10 = f32[256,2,128]{2,1,0:T(2,128)S(1)} all-to-all(f32[256,2,128]{2,1,0:T(2,128)S(1)} %bitcast.19), channel_id=1, replica_groups=mesh['leaf'=4,'dom'=64] {'leaf','dom'}, dimensions={0} | all-to-all | bytes 524288 | tf_op jit(solution)/shard_map/all_to_all | solution.py:393
  45.5 4.6 %shard_map.167 = (f32[512,128]{1,0:T(8,128)S(1)}, f32[3,150,256]{2,1,0:T(8,128)}) custom-call(f32[512,128]{1,0:T(8,128)S(1)} %bitcast.17, f32[3,125,256]{2,1,0:T(8,128)S(1)} %copy-done.2, f32[1,768]{1,0:T(1,128)S(1)} %copy-done.6, bf16[1280,256]{1,0:T(8,128)(2,1)S(1)} %copy-done, bf16[1024,128]{1,0:T(8,128)(2,1)S(1)} %copy-done.3), custom_call_target="tpu_custom_call" | custom-call | tf_op jit(solution)/shard_map/pallas_call | solution.py:364
  50.0 21.2 %all_to_all.11 = f32[256,2,128]{2,1,0:T(2,128)S(1)} all-to-all(f32[256,2,128]{2,1,0:T(2,128)S(1)} %bitcast.18), channel_id=1, replica_groups=mesh['leaf'=4,'dom'=64] {'leaf','dom'}, dimensions={0} | all-to-all | bytes 524288 | tf_op jit(solution)/shard_map/all_to_all | solution.py:405
  71.3 1.2 %shard_map.168 = f32[3,25,256]{2,1,0:T(8,128)} custom-call(f32[512,128]{1,0:T(8,128)S(1)} %bitcast.16, s32[1,256]{1,0:T(1,128)S(1)} %bitcast.22), custom_call_target="tpu_custom_call" | custom-call | tf_op jit(solution)/shard_map/pallas_call | solution.py:364
  (15 shorter events, 0.0 us)
Async XLA Ops:
  1.3 5.6 %collective-permute-start = (f32[3,125]{1,0:T(4,128)S(1)}, f32[3,125]{1,0:T(4,128)S(1)}, u32[]{:S(2)}, u32[]{:S(2)}) collective-permute-start(f32[3,125]{1,0:T(4,128)S(1)} %bitcast.30), channel_id=1, source_target_pairs={{0,1},{1,2},{2,3},{3,4},{4,5},{5,6},{6,7},{7,8},{8,9},{9,10},{10,1... | collective-permute-start | bytes 4508 | tf_op jit(solution)/shard_map/ppermute | solution.py:378
  7.0 0.7 copy-start.13
  7.0 0.7 copy-start.14
  7.0 0.7 copy-start.11
  7.0 0.7 copy-start.12
  7.0 0.7 %copy-start.9 = (s32[256]{0:T(256)S(1)}, s32[256]{0:T(256)}, u32[]{:S(2)}) copy-start(s32[256]{0:T(256)} %param.18) | copy-start | bytes 3076
  7.0 0.7 %copy-start.10 = (s32[256]{0:T(256)S(1)}, s32[256]{0:T(256)}, u32[]{:S(2)}) copy-start(s32[256]{0:T(256)} %param.19) | copy-start | bytes 3076
  7.0 0.8 %copy-start.6 = (f32[1,768]{1,0:T(1,128)S(1)}, f32[1,768]{1,0:T(1,128)}, u32[]{:S(2)}) copy-start(f32[1,768]{1,0:T(1,128)} %constant.11.clone.side_k) | copy-start | bytes 9220
  7.0 0.7 %copy-start.8 = (s32[256]{0:T(256)S(1)}, s32[256]{0:T(256)}, u32[]{:S(2)}) copy-start(s32[256]{0:T(256)} %param.17) | copy-start | bytes 3076
  7.0 0.8 %copy-start.7 = (s32[256,1]{0,1:T(1,128)S(1)}, s32[256,1]{0,1:T(1,128)}, u32[]{:S(2)}) copy-start(s32[256,1]{0,1:T(1,128)} %param.21) | copy-start | bytes 3076
  7.8 1.0 %copy-start.1 = (bf16[256,1024]{1,0:T(8,128)(2,1)S(1)}, bf16[256,1024]{1,0:T(8,128)(2,1)}, u32[]{:S(2)}) copy-start(bf16[256,1024]{1,0:T(8,128)(2,1)} %constant.10.clone.child_k) | copy-start | bytes 1572868
  8.8 0.9 %copy-start.4 = (bf16[384,256]{1,0:T(8,128)(2,1)S(1)}, bf16[384,256]{1,0:T(8,128)(2,1)}, u32[]{:S(2)}) copy-start(bf16[384,256]{1,0:T(8,128)(2,1)} %constant.12.clone.slope_k) | copy-start | bytes 589828
  9.8 0.8 %copy-start.5 = (f32[3,125,32]{1,2,0:T(8,128)S(1)}, f32[3,125,32]{1,2,0:T(8,128)}, u32[]{:S(2)}) copy-start(f32[3,125,32]{1,2,0:T(8,128)} %param.15) | copy-start | bytes 144004
  10.6 34.9 %copy-start = (bf16[1280,256]{1,0:T(8,128)(2,1)S(1)}, bf16[1280,256]{1,0:T(8,128)(2,1)}, u32[]{:S(2)}) copy-start(bf16[1280,256]{1,0:T(8,128)(2,1)} %constant.13.clone.tangent_k) | copy-start | bytes 1966084
  10.6 34.9 %copy-start.3 = (bf16[1024,128]{1,0:T(8,128)(2,1)S(1)}, bf16[1024,128]{1,0:T(8,128)(2,1)}, u32[]{:S(2)}) copy-start(bf16[1024,128]{1,0:T(8,128)(2,1)} %constant.14.clone.back_k) | copy-start | bytes 786436
  13.6 31.8 %copy-start.2 = (f32[3,125,256]{2,1,0:T(8,128)S(1)}, f32[3,125,256]{2,1,0:T(8,128)}, u32[]{:S(2)}) copy-start(f32[3,125,256]{2,1,0:T(8,128)} %coarse.1) | copy-start | bytes 1152004

commit v2 on v1

--- a/solution.py
+++ b/solution.py
@@ -324,28 +324,6 @@
     return turned[:, 1:2] * float(POOL) + turned[:, 0:1]
 
 
-def fine_kernel(slots, parents, previous, parent, octant, elem, side, owner, c_elem, c_side, quad,
-                child_k, side_k, slope_k, message_out, jac_out, pool, ints):
-    rows = [r[...].astype(F32) for r in (parent, octant, elem, side, c_elem, c_side, quad)]
-    fill_pool(pool, parents, previous)
-    keys = fill_ints(ints, *rows)
-    table = child_table(pool[...], child_k[...])
-    position = positions(owner[...].astype(F32))
-    message_out[...] = messages(table, side_matrix(side_k[...]), slots, position, ints[...])
-    jac_out[...] = determinants(table, slope_k[...], keys)[0:125]
-
-
-def mortar_kernel(message_in, coarse, side_k, tangent_k, back_k, normal_out, partial_out, scratch):
-    elements = coarse.shape[2]
-    fill_coarse(scratch, coarse)
-    faces = coarse_faces(scratch[...], side_matrix(side_k[...]))
-    message = message_in[...]
-    normal = mortar(message, faces, tangent_k[...])
-    normal_out[...] = normal
-    sums = partial_sums(normal, message, back_k[...], elements)
-    write_partials(partial_out, sums, elements)
-
-
 def write_partials(partial_out, sums, elements):
     for c in range(3):
         for s in range(6):
@@ -354,62 +332,121 @@
             ]
 
 
-def final_kernel(returned, owner, normals_out):
-    rows = face_rows(returned[...], positions(owner[...].astype(F32)))
+def everyone_else(leaves, doms, leaf, dom, act):
+    for ahead in range(leaves):
+        there = lax.rem(leaf + ahead, leaves)
+
+        def body(other, carry):
+            act(there, other)
+            return carry
+
+        lax.fori_loop(dom + 1, doms, body, 0)
+        lax.fori_loop(0, dom, body, 0)
+        if ahead:
+            act(there, dom)
+
+
+def kernel(leaves, doms, parents, previous, parent, octant, elem, side, owner, c_elem, c_side,
+           quad, coarse, child_k, side_k, slope_k, tangent_k, back_k,
+           jac_out, normals_out, partial_out,
+           pool, ints, scratch, fine_send, fine_here, normal_send, normal_here, sems):
+    leaf, dom = lax.axis_index("leaf"), lax.axis_index("dom")
+    me = leaf * doms + dom
+    ranks = leaves * doms
+    slots = 2 * ranks
+    elements = coarse.shape[2]
+    barrier = pltpu.get_barrier_semaphore()
+
+    def greet(l, d):
+        pl.semaphore_signal(
+            barrier, inc=1, device_id=(l, d), device_id_type=pl.DeviceIdType.MESH
+        )
+
+    everyone_else(leaves, doms, leaf, dom, greet)
+
+    def exchange(source, target, send_sem, recv_sem):
+        def send(l, d):
+            pltpu.make_async_remote_copy(
+                src_ref=source.at[l * doms + d],
+                dst_ref=target.at[me],
+                send_sem=send_sem,
+                recv_sem=recv_sem,
+                device_id=(l, d),
+                device_id_type=pl.DeviceIdType.MESH,
+            ).start()
+
+        everyone_else(leaves, doms, leaf, dom, send)
+        target[pl.ds(me, 1)] = source[pl.ds(me, 1)]
+
+    def wait_all(ref, sem):
+        most = ref.at[pl.ds(0, ranks - 1)]
+        pltpu.make_async_copy(most, most, sem).wait()
+
+    rows = [r[...].astype(F32) for r in (parent, octant, elem, side, c_elem, c_side, quad)]
+    fill_pool(pool, parents, previous)
+    keys = fill_ints(ints, *rows)
+    table = child_table(pool[...], child_k[...])
+    position = positions(owner[...].astype(F32))
+    sides = side_matrix(side_k[...])
+    message = messages(table, sides, slots, position, ints[...])
+    fine_send[...] = message.reshape(fine_send.shape)
+    pl.semaphore_wait(barrier, ranks - 1)
+    exchange(fine_send, fine_here, sems.at[0], sems.at[1])
+
+    jac_out[...] = determinants(table, slope_k[...], keys)[0:125]
+    fill_coarse(scratch, coarse)
+    faces = coarse_faces(scratch[...], sides)
+
+    wait_all(fine_here, sems.at[1])
+    message = fine_here[...].reshape(slots, 128)
+    normal = mortar(message, faces, tangent_k[...])
+    normal_send[...] = normal.reshape(normal_send.shape)
+    exchange(normal_send, normal_here, sems.at[2], sems.at[3])
+
+    write_partials(partial_out, partial_sums(normal, message, back_k[...], elements), elements)
+
+    wait_all(normal_here, sems.at[3])
+    returned = face_rows(normal_here[...].reshape(slots, 128), position)
     for c in range(3):
-        normals_out[c] = rows[c * 25 : c * 25 + 25]
-
-
-def call(kernel, shapes, scratch, *args):
-    return pl.pallas_call(
-        kernel,
-        out_shape=shapes,
-        scratch_shapes=scratch,
-        compiler_params=pltpu.CompilerParams(vmem_limit_bytes=48 << 20),
-    )(*args)
+        normals_out[c] = returned[c * 25 : c * 25 + 25]
+    wait_all(fine_send, sems.at[0])
+    wait_all(normal_send, sems.at[2])
 
 
 def shards(parents, coarse, parent, octant, elem, side, owner, c_elem, c_side, quad):
     axes = ("leaf", "dom")
-    ranks = lax.axis_size(axes)
-    slots = 2 * ranks
+    leaves, doms = lax.axis_size("leaf"), lax.axis_size("dom")
+    ranks = leaves * doms
     records, elements = elem.shape[0], parent.shape[0]
     row = lambda value: value.reshape(1, -1)
     previous = lax.ppermute(
         parents[:, :, -1], axes, [(source, source + 1) for source in range(ranks - 1)]
     )
-    side_k = side_constant()
-    message, jac = call(
-        functools.partial(fine_kernel, slots),
-        (
-            jax.ShapeDtypeStruct((slots, 128), F32),
+    buffer = pltpu.VMEM((ranks, 2, 128), F32)
+    return pl.pallas_call(
+        functools.partial(kernel, leaves, doms),
+        out_shape=(
             jax.ShapeDtypeStruct((125, elements), F32),
-        ),
-        [pltpu.VMEM((3 * POOL, 128), F32), pltpu.VMEM((128, records), F32)],
-        parents.transpose(0, 2, 1), previous, row(parent), row(octant), row(elem), row(side),
-        row(owner), row(c_elem), row(c_side), row(quad),
-        jnp.asarray(child_constant()), jnp.asarray(side_k), jnp.asarray(slope_constant()),
-    )
-    arrived = lax.all_to_all(message.reshape(ranks, 2, 128), axes, 0, 0, tiled=True)
-    normal, partials = call(
-        mortar_kernel,
-        (
-            jax.ShapeDtypeStruct((slots, 128), F32),
+            jax.ShapeDtypeStruct((3, 25, records), F32),
             jax.ShapeDtypeStruct((3, 150, coarse.shape[2]), F32),
         ),
-        [pltpu.VMEM((384, coarse.shape[2]), F32)],
-        arrived.reshape(slots, 128), coarse,
-        jnp.asarray(side_k), jnp.asarray(tangent_constant()),
+        scratch_shapes=[
+            pltpu.VMEM((3 * POOL, 128), F32),
+            pltpu.VMEM((128, records), F32),
+            pltpu.VMEM((384, coarse.shape[2]), F32),
+            buffer, buffer, buffer, buffer,
+            pltpu.SemaphoreType.DMA((4,)),
+        ],
+        compiler_params=pltpu.CompilerParams(
+            collective_id=0, has_side_effects=True, vmem_limit_bytes=40 << 20
+        ),
+    )(
+        parents.transpose(0, 2, 1), previous, row(parent), row(octant), row(elem), row(side),
+        row(owner), row(c_elem), row(c_side), row(quad), coarse,
+        jnp.asarray(child_constant()), jnp.asarray(side_constant()),
+        jnp.asarray(slope_constant()), jnp.asarray(tangent_constant()),
         jnp.asarray(back_constant()),
     )
-    returned = lax.all_to_all(normal.reshape(ranks, 2, 128), axes, 0, 0, tiled=True)
-    normals = call(
-        final_kernel,
-        jax.ShapeDtypeStruct((3, 25, records), F32),
-        [],
-        returned.reshape(slots, 128), row(owner),
-    )
-    return jac, normals, partials
 
 
 def solution(mesh):

time: 72.8 us -> 58.2 us (0.80)
  blocking collectives: 53.1 us -> 0 us
  Pallas kernels: 8.8 us -> 42.1 us
  local copies, waits for them, and re-layouts: 4.26 us -> 9.34 us
    all_to_all x2 -> x0, blocking collectives: 53.1 us -> none  [the longest x1 31.8 us: shards(): lax.all_to_all(message.reshape(ranks, 2, 128), axes, 0, 0, tiled=True)]
    pallas_call x3 -> x1, Pallas kernels: 8.8 us -> 42.1 us  [shards(): pl.pallas_call(functools.partial(kernel, leaves, doms), out_shape=(jax.Sh...]
    unnamed x31 -> x34, local copies, waits for them, and re-layouts: 3.54 us -> 8.63 us
where the time goes in v2:
time: 58.2 us; the launch traced here: 57.8 us
  Pallas kernels  42.1 us (72%)
  local copies, waits for them, and re-layouts  9.34 us (16%)
  starting transfers between devices  4.92 us (8%)
  waiting for transfers between devices  0.71 us (1%)
  between operations  0.7 us (1%)
    pallas_call x1, Pallas kernels, shards(): pl.pallas_call(functools.partial(kernel, leaves, doms), out_shape=(jax.Sh...  42.1 us
    unnamed x34, local copies, waits for them, and re-layouts  8.63 us
    ppermute x1, starting transfers between devices, shards(): lax.ppermute(parents[:, :, -1], axes, [(source, source + 1) for source in...  4.92 us
  transfers between devices with their start and end apart: 1, of which 1 were waited for; matrix products, arithmetic and copies ran while one was open for 0% of the time, Pallas kernels for 0%

profile of v2, /device:TPU:1, one launch (start us, length us, event | category | flops | bytes accessed | tf_op | source)
XLA Modules:
  0.0 57.8 jit_solution(8855086267624750394)
XLA Ops:
  0.6 0.7 %slice.3 = f32[3,125,1]{1,2,0:T(1,128)S(1)} slice(f32[3,125,32]{1,2,0:T(8,128)} %param.15), slice={[0:3], [0:125], [31:32]} | slice | bytes 3000 | tf_op jit(solution)/shard_map/slice | solution.py:423
  1.3 4.9 %collective-permute-start = (f32[3,125]{1,0:T(4,128)S(1)}, f32[3,125]{1,0:T(4,128)S(1)}, u32[]{:S(2)}, u32[]{:S(2)}) collective-permute-start(f32[3,125]{1,0:T(4,128)S(1)} %bitcast.21), channel_id=1, source_target_pairs={{0,1},{1,2},{2,3},{3,4},{4,5},{5,6},{6,7},{7,8},{8,9},{9,10},{10,1... | collective-permute-start | bytes 4508 | tf_op jit(solution)/shard_map/ppermute | solution.py:422
  6.3 0.7 %collective-permute-done.previous = f32[3,125]{1,0:T(4,128)S(1)} collective-permute-done((f32[3,125]{1,0:T(4,128)S(1)}, f32[3,125]{1,0:T(4,128)S(1)}, u32[]{:S(2)}, u32[]{:S(2)}) %collective-permute-start) | collective-permute-done | bytes 1532 | tf_op jit(solution)/shard_map/ppermute | solution.py:422
  7.0 0.0 copy-start.10
  7.0 0.0 copy-start.6
  7.1 0.6 %copy-done.13 = s32[256]{0:T(256)S(1)} copy-done((s32[256]{0:T(256)S(1)}, s32[256]{0:T(256)}, u32[]{:S(2)}) %copy-start.13) | copy-done | bytes 1048
  7.7 0.0 copy-done.14
  7.7 0.0 copy-done.11
  7.7 0.0 copy-done.12
  7.7 0.0 copy-done.9
  7.7 0.0 copy-done.10
  7.8 0.0 copy-done.6
  7.8 0.0 copy-done.8
  7.8 0.0 copy-done.7
  7.8 1.1 %copy-done = bf16[1280,256]{1,0:T(8,128)(2,1)S(1)} copy-done((bf16[1280,256]{1,0:T(8,128)(2,1)S(1)}, bf16[1280,256]{1,0:T(8,128)(2,1)}, u32[]{:S(2)}) %copy-start) | copy-done | bytes 655384
  8.9 1.0 %copy-done.1 = bf16[256,1024]{1,0:T(8,128)(2,1)S(1)} copy-done((bf16[256,1024]{1,0:T(8,128)(2,1)S(1)}, bf16[256,1024]{1,0:T(8,128)(2,1)}, u32[]{:S(2)}) %copy-start.1) | copy-done | bytes 524312
  9.9 1.0 %copy-done.2 = f32[3,125,256]{2,1,0:T(8,128)S(1)} copy-done((f32[3,125,256]{2,1,0:T(8,128)S(1)}, f32[3,125,256]{2,1,0:T(8,128)}, u32[]{:S(2)}) %copy-start.2) | copy-done | bytes 384024
  10.9 0.9 %copy-done.3 = bf16[1024,128]{1,0:T(8,128)(2,1)S(1)} copy-done((bf16[1024,128]{1,0:T(8,128)(2,1)S(1)}, bf16[1024,128]{1,0:T(8,128)(2,1)}, u32[]{:S(2)}) %copy-start.3) | copy-done | bytes 262168
  11.9 0.9 %copy-done.4 = bf16[384,256]{1,0:T(8,128)(2,1)S(1)} copy-done((bf16[384,256]{1,0:T(8,128)(2,1)S(1)}, bf16[384,256]{1,0:T(8,128)(2,1)}, u32[]{:S(2)}) %copy-start.4) | copy-done | bytes 196632
  12.8 0.8 %copy-done.5 = f32[3,125,32]{1,2,0:T(8,128)S(1)} copy-done((f32[3,125,32]{1,2,0:T(8,128)S(1)}, f32[3,125,32]{1,2,0:T(8,128)}, u32[]{:S(2)}) %copy-start.5) | copy-done | bytes 48024
  13.6 42.1 %shard_map.166 = (f32[125,256]{1,0:T(8,128)S(1)}, f32[3,25,256]{2,1,0:T(8,128)S(1)}, f32[3,150,256]{2,1,0:T(8,128)S(1)}) custom-call(f32[3,32,125]{2,1,0:T(8,128)S(1)} %bitcast.12, f32[3,125]{1,0:T(4,128)S(1)} %collective-permute-done.previous, s32[1,256]{1,0:T(1,128)S(1)} %bitcast.13, s32[1,256]{1,0:T(1,128)S(1)} %bitcast.14, s32[1,256]{1,0:T(1,128)S(1)} %bitcast.15, ...), custom_call_target="tpu_custom_call" | custom-call | tf_op jit(solution)/shard_map/pallas_call | solution.py:426
  55.7 0.7 %copy.25 = f32[125,256]{1,0:T(8,128)} copy(f32[125,256]{1,0:T(8,128)S(1)} %get-tuple-element.6) | data formatting | bytes 256000
  56.4 0.6 %copy.26 = f32[3,25,256]{2,1,0:T(8,128)} copy(f32[3,25,256]{2,1,0:T(8,128)S(1)} %get-tuple-element.7) | data formatting | bytes 153600
  57.0 0.8 %copy.27 = f32[3,150,256]{2,1,0:T(8,128)} copy(f32[3,150,256]{2,1,0:T(8,128)S(1)} %get-tuple-element.8) | data formatting | bytes 921600
  (14 shorter events, 0.0 us)
Async XLA Ops:
  1.3 5.6 %collective-permute-start = (f32[3,125]{1,0:T(4,128)S(1)}, f32[3,125]{1,0:T(4,128)S(1)}, u32[]{:S(2)}, u32[]{:S(2)}) collective-permute-start(f32[3,125]{1,0:T(4,128)S(1)} %bitcast.21), channel_id=1, source_target_pairs={{0,1},{1,2},{2,3},{3,4},{4,5},{5,6},{6,7},{7,8},{8,9},{9,10},{10,1... | collective-permute-start | bytes 4508 | tf_op jit(solution)/shard_map/ppermute | solution.py:422
  7.0 0.7 %copy-start.13 = (s32[256]{0:T(256)S(1)}, s32[256]{0:T(256)}, u32[]{:S(2)}) copy-start(s32[256]{0:T(256)} %param.23) | copy-start | bytes 3076
  7.0 0.7 %copy-start.14 = (s32[256]{0:T(256)S(1)}, s32[256]{0:T(256)}, u32[]{:S(2)}) copy-start(s32[256]{0:T(256)} %param.24) | copy-start | bytes 3076
  7.0 0.7 %copy-start.11 = (s32[256,1]{0,1:T(1,128)S(1)}, s32[256,1]{0,1:T(1,128)}, u32[]{:S(2)}) copy-start(s32[256,1]{0,1:T(1,128)} %param.21) | copy-start | bytes 3076
  7.0 0.7 %copy-start.12 = (s32[256]{0:T(256)S(1)}, s32[256]{0:T(256)}, u32[]{:S(2)}) copy-start(s32[256]{0:T(256)} %param.22) | copy-start | bytes 3076
  7.0 0.7 %copy-start.9 = (s32[256]{0:T(256)S(1)}, s32[256]{0:T(256)}, u32[]{:S(2)}) copy-start(s32[256]{0:T(256)} %param.19) | copy-start | bytes 3076
  7.0 0.7 %copy-start.10 = (s32[256]{0:T(256)S(1)}, s32[256]{0:T(256)}, u32[]{:S(2)}) copy-start(s32[256]{0:T(256)} %param.20) | copy-start | bytes 3076
  7.0 0.8 %copy-start.6 = (f32[1,768]{1,0:T(1,128)S(1)}, f32[1,768]{1,0:T(1,128)}, u32[]{:S(2)}) copy-start(f32[1,768]{1,0:T(1,128)} %constant.11.clone.side_k) | copy-start | bytes 9220
  7.0 0.7 %copy-start.8 = (s32[256]{0:T(256)S(1)}, s32[256]{0:T(256)}, u32[]{:S(2)}) copy-start(s32[256]{0:T(256)} %param.18) | copy-start | bytes 3076
  7.0 0.8 %copy-start.7 = (s32[256]{0:T(256)S(1)}, s32[256]{0:T(256)}, u32[]{:S(2)}) copy-start(s32[256]{0:T(256)} %param.17) | copy-start | bytes 3076
  7.8 1.1 %copy-start = (bf16[1280,256]{1,0:T(8,128)(2,1)S(1)}, bf16[1280,256]{1,0:T(8,128)(2,1)}, u32[]{:S(2)}) copy-start(bf16[1280,256]{1,0:T(8,128)(2,1)} %constant.13.clone.tangent_k) | copy-start | bytes 1966084
  8.9 1.0 %copy-start.1 = (bf16[256,1024]{1,0:T(8,128)(2,1)S(1)}, bf16[256,1024]{1,0:T(8,128)(2,1)}, u32[]{:S(2)}) copy-start(bf16[256,1024]{1,0:T(8,128)(2,1)} %constant.10.clone.child_k) | copy-start | bytes 1572868
  9.9 1.0 %copy-start.2 = (f32[3,125,256]{2,1,0:T(8,128)S(1)}, f32[3,125,256]{2,1,0:T(8,128)}, u32[]{:S(2)}) copy-start(f32[3,125,256]{2,1,0:T(8,128)} %coarse.1) | copy-start | bytes 1152004
  10.9 0.9 %copy-start.3 = (bf16[1024,128]{1,0:T(8,128)(2,1)S(1)}, bf16[1024,128]{1,0:T(8,128)(2,1)}, u32[]{:S(2)}) copy-start(bf16[1024,128]{1,0:T(8,128)(2,1)} %constant.14.clone.back_k) | copy-start | bytes 786436
  11.9 0.9 %copy-start.4 = (bf16[384,256]{1,0:T(8,128)(2,1)S(1)}, bf16[384,256]{1,0:T(8,128)(2,1)}, u32[]{:S(2)}) copy-start(bf16[384,256]{1,0:T(8,128)(2,1)} %constant.12.clone.slope_k) | copy-start | bytes 589828
  12.8 0.8 %copy-start.5 = (f32[3,125,32]{1,2,0:T(8,128)S(1)}, f32[3,125,32]{1,2,0:T(8,128)}, u32[]{:S(2)}) copy-start(f32[3,125,32]{1,2,0:T(8,128)} %param.15) | copy-start | bytes 144004

commit v3 on v2

--- a/solution.py
+++ b/solution.py
@@ -12,8 +12,9 @@
 
 F32 = jnp.float32
 BF16 = jnp.bfloat16
-POOL = 40
+POOL = 32
 MIDDLE = 62
+GROUP = 1
 VALID, ELEM, SIDE, QUAD, FSIDE, PROW, OCT = 75, 76, 77, 78, 80, 81, 82
 
 
@@ -199,39 +200,49 @@
 
 def child_table(pool, child_k):
     table = dot(triple(pool), tripled(child_k, 128))
+    count = pool.shape[0] // 3
     stacked = [
         jnp.concatenate(
-            [
-                table[c * POOL : (c + 1) * POOL, o * 128 : o * 128 + 128]
-                for c in range(3)
-            ],
-            axis=1,
+            [table[c * count : (c + 1) * count, o * 128 : o * 128 + 128] for c in range(3)], axis=1
         )
         for o in range(8)
     ]
     high, low = split(jnp.concatenate(stacked, axis=0))
-    return jnp.concatenate([high, low], axis=0)
+    return jnp.concatenate([high.astype(F32), low.astype(F32)], axis=0).astype(BF16)
 
 
 def row_picker(key, size):
-    hot = ones_where(key == iota((key.shape[0], size), 1))
-    return jnp.concatenate([hot, hot], axis=1)
-
-
-def messages(table, side_k, slots, position, ints):
-    faces = dot(table, side_k).astype(BF16)
+    places = iota((key.shape[0], 2 * size), 1)
+    places = jnp.where(places >= float(size), places - float(size), places)
+    return ones_where(key == places)
+
+
+def keys_of(parent, octant, filled):
+    own = jnp.where(filled & (parent >= 0.0), octant * float(POOL) + parent, -1.0)
+    halo = jnp.where(filled & (parent < 0.0), octant, -1.0)
+    return own, halo
+
+
+def messages(table, sides, slots, position, ints):
+    faces = dot(table, sides).astype(BF16)
     hot = ones_where(iota((slots, position.shape[1]), 0) == position)
     carried = dot_nt(hot, ints.astype(BF16))
-    filled = carried[:, VALID : VALID + 1]
-    key = carried[:, OCT : OCT + 1] * float(POOL) + carried[:, PROW : PROW + 1]
-    picker = row_picker(jnp.where(filled > 0.5, key, -1.0), 8 * POOL)
-    sides = dot(picker, faces)
-    face = pick(lane_blocks(sides, 6), carried[:, FSIDE : FSIDE + 1])
-    return jnp.where(iota(face.shape, 1) < 75.0, face, carried)
-
-
-def determinants(table, slope_k, keys):
-    children = dot(row_picker(keys, 8 * POOL), table)
+    filled = carried[:, VALID : VALID + 1] > 0.5
+    side = carried[:, FSIDE : FSIDE + 1]
+    own, halo = keys_of(carried[:, PROW : PROW + 1], carried[:, OCT : OCT + 1], filled)
+    face = pick(lane_blocks(dot(row_picker(own, 8 * POOL), faces), 6), side)
+    base = jnp.where(iota(face.shape, 1) < 75.0, face, carried)
+    return base, jnp.where(halo >= 0.0, side * 8.0 + halo, -1.0)
+
+
+def halo_messages(halo_table, sides, keys):
+    faces = dot(halo_table, sides)
+    rows = [block[8 * h : 8 * h + 8] for h in range(2) for block in lane_blocks(faces, 6)]
+    return dot(row_picker(keys, 48), jnp.concatenate(rows, axis=0).astype(BF16))
+
+
+def determinants(table, halo_table, slope_k, own, halo):
+    children = dot(row_picker(own, 8 * POOL), table) + dot(row_picker(halo, 8), halo_table)
     slope_k = tripled(slope_k, 128, 1)
     grads = [dot_nt(slope_k, triple(block)) for block in lane_blocks(children, 3)]
     g = [[grads[c][128 * d : 128 * d + 128] for c in range(3)] for d in range(3)]
@@ -290,13 +301,14 @@
     return both[:128] + both[128:]
 
 
-def fill_pool(pool, parents, previous):
+def fill_pool(pool, last, parents):
     pool[...] = jnp.zeros(pool.shape, F32)
+    last[...] = jnp.zeros(last.shape, F32)
     for c in range(3):
         own = parents[c]
-        pool[c * POOL : c * POOL + 32, 0:125] = own - own[:, MIDDLE : MIDDLE + 1]
-        last = previous[c : c + 1, 0:125]
-        pool[c * POOL + 32 : c * POOL + 33, 0:125] = last - last[:, MIDDLE : MIDDLE + 1]
+        own = own - own[:, MIDDLE : MIDDLE + 1]
+        pool[c * POOL : (c + 1) * POOL, 0:125] = own
+        last[c : c + 1, 0:125] = own[POOL - 1 :]
 
 
 def fill_coarse(scratch, coarse):
@@ -309,7 +321,6 @@
 def fill_ints(scratch, parent, octant, elem, side, c_elem, c_side, quad):
     scratch[...] = jnp.zeros(scratch.shape, F32)
     elements = parent.shape[1]
-    parent = jnp.where(parent < 0.0, 32.0, parent)
     both = jnp.concatenate([parent, octant, jnp.zeros((6, elements), F32)], axis=0)
     hot = ones_where(iota((elements, elem.shape[1]), 0) == elem)
     chosen = dot(both.astype(BF16), hot)
@@ -321,7 +332,7 @@
     scratch[PROW : PROW + 1, :] = chosen[0:1]
     scratch[OCT : OCT + 1, :] = chosen[1:2]
     turned = columns_of(both)
-    return turned[:, 1:2] * float(POOL) + turned[:, 0:1]
+    return keys_of(turned[:, 0:1], turned[:, 1:2], turned[:, 1:2] >= 0.0)
 
 
 def write_partials(partial_out, sums, elements):
@@ -332,8 +343,35 @@
             ]
 
 
-def everyone_else(leaves, doms, leaf, dom, act):
-    for ahead in range(leaves):
+INPUTS = ("parent", "octant", "elem", "owner", "side", "c_elem", "c_side", "quad", "parents",
+          "child_k", "side_k", "coarse", "slope_k", "tangent_k", "back_k")
+
+
+def kernel(leaves, doms, groups, *refs):
+    count = len(INPUTS)
+    sources = refs[:count]
+    jac_out, normals_out, partial_out = refs[count : count + 3]
+    copies = refs[count + 3 : 2 * count + 3]
+    (pool, last, halo_in, ints, scratch, fine_send, fine_here, normal_send, normal_here,
+     in_sems, halo_sems, send_sems, fine_sems, normal_sems) = refs[2 * count + 3 :]
+    leaf, dom = lax.axis_index("leaf"), lax.axis_index("dom")
+    ranks = leaves * doms
+    me = leaf * doms + dom
+    slots = 2 * ranks
+    mesh_id = pl.DeviceIdType.MESH
+
+    loads = {
+        name: pltpu.make_async_copy(sources[at], copies[at], in_sems.at[at])
+        for at, name in enumerate(INPUTS)
+    }
+    for name in INPUTS:
+        loads[name].start()
+
+    def load(name):
+        loads[name].wait()
+        return copies[INPUTS.index(name)]
+
+    def others(ahead, act):
         there = lax.rem(leaf + ahead, leaves)
 
         def body(other, carry):
@@ -345,26 +383,15 @@
         if ahead:
             act(there, dom)
 
-
-def kernel(leaves, doms, parents, previous, parent, octant, elem, side, owner, c_elem, c_side,
-           quad, coarse, child_k, side_k, slope_k, tangent_k, back_k,
-           jac_out, normals_out, partial_out,
-           pool, ints, scratch, fine_send, fine_here, normal_send, normal_here, sems):
-    leaf, dom = lax.axis_index("leaf"), lax.axis_index("dom")
-    me = leaf * doms + dom
-    ranks = leaves * doms
-    slots = 2 * ranks
-    elements = coarse.shape[2]
     barrier = pltpu.get_barrier_semaphore()
 
     def greet(l, d):
-        pl.semaphore_signal(
-            barrier, inc=1, device_id=(l, d), device_id_type=pl.DeviceIdType.MESH
-        )
-
-    everyone_else(leaves, doms, leaf, dom, greet)
-
-    def exchange(source, target, send_sem, recv_sem):
+        pl.semaphore_signal(barrier, inc=1, device_id=(l, d), device_id_type=mesh_id)
+
+    for ahead in range(leaves):
+        others(ahead, greet)
+
+    def send_all(ahead, source, target, send_sem, recv_sem):
         def send(l, d):
             pltpu.make_async_remote_copy(
                 src_ref=source.at[l * doms + d],
@@ -372,81 +399,145 @@
                 send_sem=send_sem,
                 recv_sem=recv_sem,
                 device_id=(l, d),
-                device_id_type=pl.DeviceIdType.MESH,
+                device_id_type=mesh_id,
             ).start()
 
-        everyone_else(leaves, doms, leaf, dom, send)
-        target[pl.ds(me, 1)] = source[pl.ds(me, 1)]
-
-    def wait_all(ref, sem):
-        most = ref.at[pl.ds(0, ranks - 1)]
+        others(ahead, send)
+
+    def wait_rows(ref, rows, sem):
+        most = ref.at[pl.ds(0, rows)]
         pltpu.make_async_copy(most, most, sem).wait()
 
-    rows = [r[...].astype(F32) for r in (parent, octant, elem, side, c_elem, c_side, quad)]
-    fill_pool(pool, parents, previous)
-    keys = fill_ints(ints, *rows)
-    table = child_table(pool[...], child_k[...])
-    position = positions(owner[...].astype(F32))
-    sides = side_matrix(side_k[...])
-    message = messages(table, sides, slots, position, ints[...])
+    def wait_leaf(ref, back, sems):
+        wait_rows(ref, doms if back else doms - 1, sems.at[back])
+
+    names = ("parent", "octant", "elem", "side", "c_elem", "c_side", "quad")
+    own_keys, halo_keys = fill_ints(ints, *[load(name)[...].astype(F32) for name in names])
+    position = positions(load("owner")[...].astype(F32))
+    fill_pool(pool, last, load("parents"))
+    child_k = load("child_k")[...]
+    table = child_table(pool[...], child_k)
+    sides = side_matrix(load("side_k")[...])
+    message, message_keys = messages(table, sides, slots, position, ints[...])
+
+    pl.semaphore_wait(barrier, ranks - 1)
+    after = lax.rem(me + 1, ranks)
+    halo = pltpu.make_async_remote_copy(
+        src_ref=last,
+        dst_ref=halo_in,
+        send_sem=halo_sems.at[0],
+        recv_sem=halo_sems.at[1],
+        device_id=(after // doms, lax.rem(after, doms)),
+        device_id_type=mesh_id,
+    )
+    halo.start()
+    scratch_ref = load("coarse")
+    elements = scratch_ref.shape[2]
+    fill_coarse(scratch, scratch_ref)
+    faces = coarse_faces(scratch[...], sides)
+    halo.wait()
+    halo_table = child_table(jnp.concatenate([halo_in[c : c + 1] for c in range(3)], axis=0), child_k)
+    message = message + halo_messages(halo_table, sides, message_keys)
     fine_send[...] = message.reshape(fine_send.shape)
-    pl.semaphore_wait(barrier, ranks - 1)
-    exchange(fine_send, fine_here, sems.at[0], sems.at[1])
-
-    jac_out[...] = determinants(table, slope_k[...], keys)[0:125]
-    fill_coarse(scratch, coarse)
-    faces = coarse_faces(scratch[...], sides)
-
-    wait_all(fine_here, sems.at[1])
+    for ahead in range(leaves):
+        send_all(ahead, fine_send, fine_here, send_sems.at[0], fine_sems.at[ahead])
+    fine_here[pl.ds(me, 1)] = fine_send[pl.ds(me, 1)]
+
+    slope_k = load("slope_k")[...]
+    jac_out[...] = determinants(table, halo_table, slope_k, own_keys, halo_keys)[0:125]
+    tangent_k = load("tangent_k")[...]
+    back_k = load("back_k")[...]
+
+    for group in groups:
+        starts = [lax.rem(leaf + leaves - back, leaves) * doms for back in group]
+        for back in group:
+            wait_leaf(fine_here, back, fine_sems)
+        rows = [fine_here[pl.ds(start, doms)].reshape(2 * doms, 128) for start in starts]
+        normal = mortar(jnp.concatenate(rows, axis=0), faces, tangent_k)
+        for number, (back, start) in enumerate(zip(group, starts)):
+            mine = normal[number * 2 * doms : (number + 1) * 2 * doms]
+            normal_send[pl.ds(start, doms)] = mine.reshape(doms, 2, 128)
+        for back in group:
+            send_all(
+                (leaves - back) % leaves, normal_send, normal_here, send_sems.at[1],
+                normal_sems.at[(leaves - back) % leaves],
+            )
+    normal_here[pl.ds(me, 1)] = normal_send[pl.ds(me, 1)]
+
+    normal = normal_send[...].reshape(slots, 128)
     message = fine_here[...].reshape(slots, 128)
-    normal = mortar(message, faces, tangent_k[...])
-    normal_send[...] = normal.reshape(normal_send.shape)
-    exchange(normal_send, normal_here, sems.at[2], sems.at[3])
-
-    write_partials(partial_out, partial_sums(normal, message, back_k[...], elements), elements)
-
-    wait_all(normal_here, sems.at[3])
+    write_partials(partial_out, partial_sums(normal, message, back_k, elements), elements)
+
+    for back in range(leaves):
+        wait_leaf(normal_here, back, normal_sems)
     returned = face_rows(normal_here[...].reshape(slots, 128), position)
     for c in range(3):
         normals_out[c] = returned[c * 25 : c * 25 + 25]
-    wait_all(fine_send, sems.at[0])
-    wait_all(normal_send, sems.at[2])
+    wait_rows(fine_send, ranks - 1, send_sems.at[0])
+    wait_rows(normal_send, ranks - 1, send_sems.at[1])
+
+
+def store_kernel(*refs):
+    count = (len(refs) - 1) // 2
+    copies = [
+        pltpu.make_async_copy(refs[at], refs[count + at], refs[-1].at[at]) for at in range(count)
+    ]
+    for copy in copies:
+        copy.start()
+    for copy in copies:
+        copy.wait()
 
 
 def shards(parents, coarse, parent, octant, elem, side, owner, c_elem, c_side, quad):
-    axes = ("leaf", "dom")
     leaves, doms = lax.axis_size("leaf"), lax.axis_size("dom")
     ranks = leaves * doms
     records, elements = elem.shape[0], parent.shape[0]
     row = lambda value: value.reshape(1, -1)
-    previous = lax.ppermute(
-        parents[:, :, -1], axes, [(source, source + 1) for source in range(ranks - 1)]
+    given = dict(
+        parent=row(parent), octant=row(octant), elem=row(elem), side=row(side), owner=row(owner),
+        c_elem=row(c_elem), c_side=row(c_side), quad=row(quad),
+        parents=parents.transpose(0, 2, 1), coarse=coarse,
+        child_k=jnp.asarray(child_constant()), side_k=jnp.asarray(side_constant()),
+        slope_k=jnp.asarray(slope_constant()), tangent_k=jnp.asarray(tangent_constant()),
+        back_k=jnp.asarray(back_constant()),
     )
+    args = [given[name] for name in INPUTS]
     buffer = pltpu.VMEM((ranks, 2, 128), F32)
-    return pl.pallas_call(
-        functools.partial(kernel, leaves, doms),
-        out_shape=(
-            jax.ShapeDtypeStruct((125, elements), F32),
-            jax.ShapeDtypeStruct((3, 25, records), F32),
-            jax.ShapeDtypeStruct((3, 150, coarse.shape[2]), F32),
-        ),
-        scratch_shapes=[
+    groups = [list(range(leaves))[at : at + GROUP] for at in range(0, leaves, GROUP)]
+    shapes = (
+        jax.ShapeDtypeStruct((125, elements), F32),
+        jax.ShapeDtypeStruct((3, 25, records), F32),
+        jax.ShapeDtypeStruct((3, 150, coarse.shape[2]), F32),
+    )
+    results = pl.pallas_call(
+        functools.partial(kernel, leaves, doms, groups),
+        out_shape=shapes,
+        in_specs=[pl.BlockSpec(memory_space=pltpu.HBM)] * len(args),
+        out_specs=[pl.BlockSpec(memory_space=pltpu.VMEM)] * 3,
+        scratch_shapes=[pltpu.VMEM(arg.shape, arg.dtype) for arg in args] + [
             pltpu.VMEM((3 * POOL, 128), F32),
+            pltpu.VMEM((8, 128), F32),
+            pltpu.VMEM((8, 128), F32),
             pltpu.VMEM((128, records), F32),
             pltpu.VMEM((384, coarse.shape[2]), F32),
             buffer, buffer, buffer, buffer,
-            pltpu.SemaphoreType.DMA((4,)),
+            pltpu.SemaphoreType.DMA((len(args),)),
+            pltpu.SemaphoreType.DMA((2,)),
+            pltpu.SemaphoreType.DMA((2,)),
+            pltpu.SemaphoreType.DMA((leaves,)),
+            pltpu.SemaphoreType.DMA((leaves,)),
         ],
         compiler_params=pltpu.CompilerParams(
-            collective_id=0, has_side_effects=True, vmem_limit_bytes=40 << 20
+            collective_id=0, has_side_effects=True
         ),
-    )(
-        parents.transpose(0, 2, 1), previous, row(parent), row(octant), row(elem), row(side),
-        row(owner), row(c_elem), row(c_side), row(quad), coarse,
-        jnp.asarray(child_constant()), jnp.asarray(side_constant()),
-        jnp.asarray(slope_constant()), jnp.asarray(tangent_constant()),
-        jnp.asarray(back_constant()),
-    )
+    )(*args)
+    return pl.pallas_call(
+        store_kernel,
+        out_shape=shapes,
+        in_specs=[pl.BlockSpec(memory_space=pltpu.VMEM)] * 3,
+        out_specs=[pl.BlockSpec(memory_space=pltpu.HBM)] * 3,
+        scratch_shapes=[pltpu.SemaphoreType.DMA((3,))],
+    )(*results)
 
 
 def solution(mesh):

time: 58.2 us -> 44 us (0.76)
  local copies, waits for them, and re-layouts: 9.34 us -> 0 us
  starting transfers between devices: 4.92 us -> 0 us
  Pallas kernels: 42.1 us -> 43.1 us
  waiting for transfers between devices: 0.71 us -> 0 us
    unnamed x34 -> x0, local copies, waits for them, and re-layouts: 8.63 us -> none
    ppermute x1 -> x0, starting transfers between devices: 4.92 us -> none  [shards(): lax.ppermute(parents[:, :, -1], axes, [(source, source + 1) for source in...]
    pallas_call x1 -> x2, Pallas kernels: 42.1 us -> 43.1 us  [the longest x1 41.1 us: shards(): pl.pallas_call(functools.partial(kernel, leaves, doms, groups), out_shape...]
    slice x1 -> x0, local copies, waits for them, and re-layouts: 0.71 us -> none  [shards(): parents[:, :, -1]]
    ppermute x1 -> x0, waiting for transfers between devices: 0.71 us -> none  [shards(): lax.ppermute(parents[:, :, -1], axes, [(source, source + 1) for source in...]
  transfers between devices with their start and end apart: 1 -> 0, of which waited for: 1 -> 0; matrix products, arithmetic and copies ran while one was open for 0% -> 0% of each run, Pallas kernels for 0% -> 0%
where the time goes in v3:
time: 44 us; the launch traced here: 43.9 us
  Pallas kernels  43.1 us (98%)
  between operations  0.8 us (2%)
    pallas_call x1, Pallas kernels, shards(): pl.pallas_call(functools.partial(kernel, leaves, doms, groups), out_shape...  41.1 us
    pallas_call x1, Pallas kernels, shards(): pl.pallas_call(store_kernel, out_shape=shapes, in_specs=[pl.BlockSpec(mem...  2.01 us

profile of v3, /device:TPU:1, one launch (start us, length us, event | category | flops | bytes accessed | tf_op | source)
XLA Modules:
  0.0 43.9 jit_solution(2010263906694511183)
XLA Ops:
  0.6 41.1 %shard_map.166 = (f32[125,256]{1,0:T(8,128)}, f32[3,25,256]{2,1,0:T(8,128)}, f32[3,150,256]{2,1,0:T(8,128)}) custom-call(s32[1,256]{1,0:T(1,128)} %bitcast.10, s32[1,256]{1,0:T(1,128)} %bitcast.11, s32[1,256]{1,0:T(1,128)} %bitcast.12, s32[1,256]{1,0:T(1,128)} %bitcast.13, s32[1,256]{1,0:T(1,128)} %bitcast.14, s32[1,256]{1,0:T(1,128)} %bitcast.15, ...), custom_call_target="tpu_custom_call" | custom-call | tf_op jit(solution)/shard_map/pallas_call | solution.py:512
  41.7 2.0 %shard_map.167 = (f32[125,256]{1,0:T(8,128)}, f32[3,25,256]{2,1,0:T(8,128)}, f32[3,150,256]{2,1,0:T(8,128)}) custom-call(f32[125,256]{1,0:T(8,128)} %get-tuple-element.6.refs_0_, f32[3,25,256]{2,1,0:T(8,128)} %get-tuple-element.7.refs_1_, f32[3,150,256]{2,1,0:T(8,128)} %get-tuple-element.8.refs_2_), custom_call_target="tpu_custom_call" | custom-call | tf_op jit(solution)/shard_map/pallas_call | solution.py:534

commit v4 on v3

--- a/solution.py
+++ b/solution.py
@@ -371,24 +371,42 @@
         loads[name].wait()
         return copies[INPUTS.index(name)]
 
+    xs = max(doms // 16, 1)
+    zs = doms // (2 * xs)
+    at_x, at_z, core = dom // (2 * zs), lax.rem(dom // 2, zs), lax.rem(dom, 2)
+    z_steps = sorted(range(zs), key=lambda step: -min(step, zs - step))
+    by_z = [(step, lax.rem(at_z + step, zs) * 2) for step in z_steps]
+    by_core = [(1, 1 - core), (0, core)]
+
     def others(ahead, act):
         there = lax.rem(leaf + ahead, leaves)
 
-        def body(other, carry):
-            act(there, other)
+        def plane(step_x, skip):
+            base = lax.rem(at_x + step_x, xs) * (2 * zs)
+            for step_z, z_part in by_z:
+                for step_core, core_part in by_core:
+                    if not (skip and step_z == 0 and step_core == 0):
+                        act(there, base + z_part + core_part)
+
+        def body(number, carry):
+            plane(number + xs // 2, False)
             return carry
 
-        lax.fori_loop(dom + 1, doms, body, 0)
-        lax.fori_loop(0, dom, body, 0)
         if ahead:
-            act(there, dom)
+            lax.fori_loop(0, xs, body, 0)
+        else:
+            for number in range(xs):
+                step_x = (number + xs // 2) % xs
+                plane(step_x, step_x == 0)
+
+    far_first = sorted(range(leaves), key=lambda step: -min(step, leaves - step))
 
     barrier = pltpu.get_barrier_semaphore()
 
     def greet(l, d):
         pl.semaphore_signal(barrier, inc=1, device_id=(l, d), device_id_type=mesh_id)
 
-    for ahead in range(leaves):
+    for ahead in far_first:
         others(ahead, greet)
 
     def send_all(ahead, source, target, send_sem, recv_sem):
@@ -439,7 +457,7 @@
     halo_table = child_table(jnp.concatenate([halo_in[c : c + 1] for c in range(3)], axis=0), child_k)
     message = message + halo_messages(halo_table, sides, message_keys)
     fine_send[...] = message.reshape(fine_send.shape)
-    for ahead in range(leaves):
+    for ahead in far_first:
         send_all(ahead, fine_send, fine_here, send_sems.at[0], fine_sems.at[ahead])
     fine_here[pl.ds(me, 1)] = fine_send[pl.ds(me, 1)]
 
@@ -477,17 +495,6 @@
     wait_rows(normal_send, ranks - 1, send_sems.at[1])
 
 
-def store_kernel(*refs):
-    count = (len(refs) - 1) // 2
-    copies = [
-        pltpu.make_async_copy(refs[at], refs[count + at], refs[-1].at[at]) for at in range(count)
-    ]
-    for copy in copies:
-        copy.start()
-    for copy in copies:
-        copy.wait()
-
-
 def shards(parents, coarse, parent, octant, elem, side, owner, c_elem, c_side, quad):
     leaves, doms = lax.axis_size("leaf"), lax.axis_size("dom")
     ranks = leaves * doms
@@ -501,15 +508,16 @@
         slope_k=jnp.asarray(slope_constant()), tangent_k=jnp.asarray(tangent_constant()),
         back_k=jnp.asarray(back_constant()),
     )
-    args = [given[name] for name in INPUTS]
+    args = [pltpu.with_memory_space_constraint(given[name], pltpu.HBM) for name in INPUTS]
     buffer = pltpu.VMEM((ranks, 2, 128), F32)
-    groups = [list(range(leaves))[at : at + GROUP] for at in range(0, leaves, GROUP)]
+    far_first = sorted(range(leaves), key=lambda step: -min(step, leaves - step))
+    groups = [far_first[at : at + GROUP] for at in range(0, leaves, GROUP)]
     shapes = (
         jax.ShapeDtypeStruct((125, elements), F32),
         jax.ShapeDtypeStruct((3, 25, records), F32),
         jax.ShapeDtypeStruct((3, 150, coarse.shape[2]), F32),
     )
-    results = pl.pallas_call(
+    return pl.pallas_call(
         functools.partial(kernel, leaves, doms, groups),
         out_shape=shapes,
         in_specs=[pl.BlockSpec(memory_space=pltpu.HBM)] * len(args),
@@ -528,16 +536,9 @@
             pltpu.SemaphoreType.DMA((leaves,)),
         ],
         compiler_params=pltpu.CompilerParams(
-            collective_id=0, has_side_effects=True
+            collective_id=0, has_side_effects=True, vmem_limit_bytes=40 << 20
         ),
     )(*args)
-    return pl.pallas_call(
-        store_kernel,
-        out_shape=shapes,
-        in_specs=[pl.BlockSpec(memory_space=pltpu.VMEM)] * 3,
-        out_specs=[pl.BlockSpec(memory_space=pltpu.HBM)] * 3,
-        scratch_shapes=[pltpu.SemaphoreType.DMA((3,))],
-    )(*results)
 
 
 def solution(mesh):

time: 44 us -> 40.8 us (0.927)
  Pallas kernels: 43.1 us -> 38 us
  local copies, waits for them, and re-layouts: 0 us -> 2.07 us
    pallas_call x1, Pallas kernels: 41.1 us -> 38 us  [shards(): pl.pallas_call(functools.partial(kernel, leaves, doms, groups), out_shape...]
    unnamed x0 -> x3, local copies, waits for them, and re-layouts: none -> 2.07 us
    pallas_call x1 -> x0, Pallas kernels: 2.01 us -> none  [shards(): pl.pallas_call(store_kernel, out_shape=shapes, in_specs=[pl.BlockSpec(mem...]
where the time goes in v4:
time: 40.8 us; the launch traced here: 40.7 us
  Pallas kernels  38 us (93%)
  local copies, waits for them, and re-layouts  2.07 us (5%)
  between operations  0.64 us (2%)
    pallas_call x1, Pallas kernels, shards(): pl.pallas_call(functools.partial(kernel, leaves, doms, groups), out_shape...  38 us
    unnamed x3, local copies, waits for them, and re-layouts  2.07 us

profile of v4, /device:TPU:1, one launch (start us, length us, event | category | flops | bytes accessed | tf_op | source)
XLA Modules:
  0.0 40.7 jit_solution(10954109643394805424)
XLA Ops:
  0.6 38.0 %shard_map.166 = (f32[125,256]{1,0:T(8,128)S(1)}, f32[3,25,256]{2,1,0:T(8,128)S(1)}, f32[3,150,256]{2,1,0:T(8,128)S(1)}) custom-call(s32[1,256]{1,0:T(1,128)} %bitcast.10, s32[1,256]{1,0:T(1,128)} %bitcast.11, s32[1,256]{1,0:T(1,128)} %bitcast.12, s32[1,256]{1,0:T(1,128)} %bitcast.13, s32[1,256]{1,0:T(1,128)} %bitcast.14, s32[1,256]{1,0:T(1,128)} %bitcast.15, ...), custom_call_target="tpu_custom_call" | custom-call | tf_op jit(solution)/shard_map/pallas_call | solution.py:520
  38.7 0.7 %copy.21 = f32[125,256]{1,0:T(8,128)} copy(f32[125,256]{1,0:T(8,128)S(1)} %get-tuple-element.6) | data formatting | bytes 256000
  39.3 0.6 %copy.22 = f32[3,25,256]{2,1,0:T(8,128)} copy(f32[3,25,256]{2,1,0:T(8,128)S(1)} %get-tuple-element.7) | data formatting | bytes 153600
  40.0 0.8 %copy.23 = f32[3,150,256]{2,1,0:T(8,128)} copy(f32[3,150,256]{2,1,0:T(8,128)S(1)} %get-tuple-element.8) | data formatting | bytes 921600

commit v5 on v4

--- a/solution.py
+++ b/solution.py
@@ -15,7 +15,8 @@
 POOL = 32
 MIDDLE = 62
 GROUP = 1
-VALID, ELEM, SIDE, QUAD, FSIDE, PROW, OCT = 75, 76, 77, 78, 80, 81, 82
+VALID, ELEM, SIDE, QUAD, FSIDE, PROW, OCT = range(7)
+SECOND = 64
 
 
 def lobatto_nodes():
@@ -223,16 +224,37 @@
     return own, halo
 
 
-def messages(table, sides, slots, position, ints):
+def slot_integers(ints, slots, position):
+    hot = ones_where(iota((slots, position.shape[1]), 0) == position)
+    return dot_nt(hot, ints.astype(BF16))
+
+
+def requests(ints, pairs, position, scratch):
+    records = ints.shape[1]
+    scratch[...] = jnp.zeros(scratch.shape, F32)
+    scratch[0:8, 0:records] = ints
+    scratch[SECOND : SECOND + 8, records : 2 * records] = ints
+    places = iota((pairs, records), 0) * 2.0
+    hot = jnp.concatenate([ones_where(places == position), ones_where(places + 1.0 == position)], 1)
+    return dot_nt(hot, scratch[...].astype(BF16))
+
+
+def expanded(rows):
+    pairs = rows.shape[0]
+    slot, pair = iota((2 * pairs, pairs), 0), iota((2 * pairs, pairs), 1)
+    first, second = ones_where(slot == 2.0 * pair), ones_where(slot == 2.0 * pair + 1.0)
+    rows = rows.astype(BF16)
+    both = dot(first, rows), pltpu.roll(dot(second, rows), SECOND, 1)
+    return both[0] + both[1]
+
+
+def messages(table, sides, carried):
     faces = dot(table, sides).astype(BF16)
-    hot = ones_where(iota((slots, position.shape[1]), 0) == position)
-    carried = dot_nt(hot, ints.astype(BF16))
     filled = carried[:, VALID : VALID + 1] > 0.5
     side = carried[:, FSIDE : FSIDE + 1]
     own, halo = keys_of(carried[:, PROW : PROW + 1], carried[:, OCT : OCT + 1], filled)
     face = pick(lane_blocks(dot(row_picker(own, 8 * POOL), faces), 6), side)
-    base = jnp.where(iota(face.shape, 1) < 75.0, face, carried)
-    return base, jnp.where(halo >= 0.0, side * 8.0 + halo, -1.0)
+    return face, jnp.where(halo >= 0.0, side * 8.0 + halo, -1.0)
 
 
 def halo_messages(halo_table, sides, keys):
@@ -257,32 +279,30 @@
     return jnp.concatenate([dot(high, side_k), dot(low, side_k)], axis=1).astype(BF16)
 
 
-def mortar(message, faces, tangent_k):
-    slots = message.shape[0]
-    elements = faces.shape[0]
-    filled = message[:, VALID : VALID + 1] > 0.5
-    elem = jnp.where(filled, message[:, ELEM : ELEM + 1], -1.0)
-    side, quad = message[:, SIDE : SIDE + 1], message[:, QUAD : QUAD + 1]
-    hot = ones_where(elem == iota((slots, elements), 1))
+def coarse_rows(integers, faces):
+    filled = integers[:, VALID : VALID + 1] > 0.5
+    elem = jnp.where(filled, integers[:, ELEM : ELEM + 1], -1.0)
+    side = integers[:, SIDE : SIDE + 1]
+    hot = ones_where(elem == iota((integers.shape[0], faces.shape[0]), 1))
     blocks = lane_blocks(dot(hot, faces), 12)
-    high, low = pick(blocks[:6], side), pick(blocks[6:], side)
-    parts = [triple(message)]
+    return pick(blocks[:6], side) + pick(blocks[6:], side)
+
+
+def mortar(fine, coarse, quad, tangent_k):
+    parts = [triple(fine)]
     for number in range(4):
-        mine = quad == float(number)
-        this_high = jnp.where(mine, high, 0.0).astype(BF16)
-        this_low = jnp.where(mine, low, 0.0).astype(BF16)
-        parts += [this_high, this_low, this_high]
+        parts.append(triple(jnp.where(quad == float(number), coarse, 0.0)))
     tangents = dot(jnp.concatenate(parts, axis=1), tripled(tangent_k, 128))
     t1, t2 = tangents[:, :128], tangents[:, 128:]
     ahead = lambda value, count: pltpu.roll(value, 128 - 25 * count, 1)
     return ahead(t1, 1) * ahead(t2, 2) - ahead(t1, 2) * ahead(t2, 1)
 
 
-def partial_sums(normal, message, back_k, elements):
-    slots = message.shape[0]
-    filled = message[:, VALID : VALID + 1] > 0.5
-    side, quad = message[:, SIDE : SIDE + 1], message[:, QUAD : QUAD + 1]
-    key = side * float(elements) + message[:, ELEM : ELEM + 1]
+def partial_sums(normal, integers, back_k, elements):
+    slots = integers.shape[0]
+    filled = integers[:, VALID : VALID + 1] > 0.5
+    side, quad = integers[:, SIDE : SIDE + 1], integers[:, QUAD : QUAD + 1]
+    key = side * float(elements) + integers[:, ELEM : ELEM + 1]
     key = jnp.where(filled, key, -1.0)
     parts = []
     for number in range(4):
@@ -318,21 +338,16 @@
         scratch[c * 128 : c * 128 + 125, :] = whole - whole[MIDDLE : MIDDLE + 1]
 
 
-def fill_ints(scratch, parent, octant, elem, side, c_elem, c_side, quad):
-    scratch[...] = jnp.zeros(scratch.shape, F32)
+def record_integers(parent, octant, elem, side, c_elem, c_side, quad):
     elements = parent.shape[1]
     both = jnp.concatenate([parent, octant, jnp.zeros((6, elements), F32)], axis=0)
     hot = ones_where(iota((elements, elem.shape[1]), 0) == elem)
     chosen = dot(both.astype(BF16), hot)
-    scratch[VALID : VALID + 1, :] = jnp.ones_like(elem)
-    scratch[ELEM : ELEM + 1, :] = c_elem
-    scratch[SIDE : SIDE + 1, :] = c_side
-    scratch[QUAD : QUAD + 1, :] = quad
-    scratch[FSIDE : FSIDE + 1, :] = side
-    scratch[PROW : PROW + 1, :] = chosen[0:1]
-    scratch[OCT : OCT + 1, :] = chosen[1:2]
+    rows = [jnp.ones_like(elem), c_elem, c_side, quad, side, chosen[0:1], chosen[1:2],
+            jnp.zeros_like(elem)]
     turned = columns_of(both)
-    return keys_of(turned[:, 0:1], turned[:, 1:2], turned[:, 1:2] >= 0.0)
+    keys = keys_of(turned[:, 0:1], turned[:, 1:2], turned[:, 1:2] >= 0.0)
+    return jnp.concatenate(rows, axis=0), keys
 
 
 def write_partials(partial_out, sums, elements):
@@ -352,8 +367,9 @@
     sources = refs[:count]
     jac_out, normals_out, partial_out = refs[count : count + 3]
     copies = refs[count + 3 : 2 * count + 3]
-    (pool, last, halo_in, ints, scratch, fine_send, fine_here, normal_send, normal_here,
-     in_sems, halo_sems, send_sems, fine_sems, normal_sems) = refs[2 * count + 3 :]
+    (pool, last, halo_in, wide, scratch, ask_send, ask_here, fine_send, fine_here,
+     coarse_send, coarse_here,
+     in_sems, halo_sems, send_sems, ask_sems, fine_sems, coarse_sems) = refs[2 * count + 3 :]
     leaf, dom = lax.axis_index("leaf"), lax.axis_index("dom")
     ranks = leaves * doms
     me = leaf * doms + dom
@@ -430,13 +446,15 @@
         wait_rows(ref, doms if back else doms - 1, sems.at[back])
 
     names = ("parent", "octant", "elem", "side", "c_elem", "c_side", "quad")
-    own_keys, halo_keys = fill_ints(ints, *[load(name)[...].astype(F32) for name in names])
+    ints, keys = record_integers(*[load(name)[...].astype(F32) for name in names])
     position = positions(load("owner")[...].astype(F32))
+    ask_send[...] = requests(ints, ranks, position, wide).reshape(ask_send.shape)
+    carried = slot_integers(ints, slots, position)
     fill_pool(pool, last, load("parents"))
     child_k = load("child_k")[...]
     table = child_table(pool[...], child_k)
     sides = side_matrix(load("side_k")[...])
-    message, message_keys = messages(table, sides, slots, position, ints[...])
+    fine, fine_keys = messages(table, sides, carried)
 
     pl.semaphore_wait(barrier, ranks - 1)
     after = lax.rem(me + 1, ranks)
@@ -449,50 +467,65 @@
         device_id_type=mesh_id,
     )
     halo.start()
-    scratch_ref = load("coarse")
-    elements = scratch_ref.shape[2]
-    fill_coarse(scratch, scratch_ref)
-    faces = coarse_faces(scratch[...], sides)
+    for ahead in far_first:
+        send_all(ahead, ask_send, ask_here, send_sems.at[0], ask_sems.at[ahead])
+    ask_here[pl.ds(me, 1)] = ask_send[pl.ds(me, 1)]
     halo.wait()
     halo_table = child_table(jnp.concatenate([halo_in[c : c + 1] for c in range(3)], axis=0), child_k)
-    message = message + halo_messages(halo_table, sides, message_keys)
-    fine_send[...] = message.reshape(fine_send.shape)
+    fine = fine + halo_messages(halo_table, sides, fine_keys)
+    fine_send[...] = fine.reshape(fine_send.shape)
     for ahead in far_first:
-        send_all(ahead, fine_send, fine_here, send_sems.at[0], fine_sems.at[ahead])
+        send_all(ahead, fine_send, fine_here, send_sems.at[1], fine_sems.at[ahead])
     fine_here[pl.ds(me, 1)] = fine_send[pl.ds(me, 1)]
 
-    slope_k = load("slope_k")[...]
-    jac_out[...] = determinants(table, halo_table, slope_k, own_keys, halo_keys)[0:125]
+    coarse = load("coarse")
+    elements = coarse.shape[2]
+    fill_coarse(scratch, coarse)
+    faces = coarse_faces(scratch[...], sides)
     tangent_k = load("tangent_k")[...]
     back_k = load("back_k")[...]
-
+    slope_k = load("slope_k")[...]
+
+    asked = []
     for group in groups:
         starts = [lax.rem(leaf + leaves - back, leaves) * doms for back in group]
         for back in group:
-            wait_leaf(fine_here, back, fine_sems)
-        rows = [fine_here[pl.ds(start, doms)].reshape(2 * doms, 128) for start in starts]
-        normal = mortar(jnp.concatenate(rows, axis=0), faces, tangent_k)
-        for number, (back, start) in enumerate(zip(group, starts)):
-            mine = normal[number * 2 * doms : (number + 1) * 2 * doms]
-            normal_send[pl.ds(start, doms)] = mine.reshape(doms, 2, 128)
+            wait_leaf(ask_here, back, ask_sems)
+        for start in starts:
+            rows = ask_here[pl.ds(start, doms)].reshape(doms, 128)
+            asked.append(expanded(rows))
+        rows = coarse_rows(jnp.concatenate(asked[-len(group) :], axis=0), faces)
+        for number, start in enumerate(starts):
+            mine = rows[number * 2 * doms : (number + 1) * 2 * doms]
+            coarse_send[pl.ds(start, doms)] = mine.reshape(doms, 2, 128)
         for back in group:
-            send_all(
-                (leaves - back) % leaves, normal_send, normal_here, send_sems.at[1],
-                normal_sems.at[(leaves - back) % leaves],
-            )
-    normal_here[pl.ds(me, 1)] = normal_send[pl.ds(me, 1)]
-
-    normal = normal_send[...].reshape(slots, 128)
-    message = fine_here[...].reshape(slots, 128)
-    write_partials(partial_out, partial_sums(normal, message, back_k, elements), elements)
-
-    for back in range(leaves):
-        wait_leaf(normal_here, back, normal_sems)
-    returned = face_rows(normal_here[...].reshape(slots, 128), position)
+            ahead = (leaves - back) % leaves
+            send_all(ahead, coarse_send, coarse_here, send_sems.at[2], coarse_sems.at[ahead])
+    coarse_here[pl.ds(me, 1)] = coarse_send[pl.ds(me, 1)]
+
+    jac_out[...] = determinants(table, halo_table, slope_k, *keys)[0:125]
+
+    order = [back for group in groups for back in group]
+    starts = [lax.rem(leaf + leaves - back, leaves) * doms for back in order]
+    part = lambda ref: jnp.concatenate(
+        [ref[pl.ds(start, doms)].reshape(2 * doms, 128) for start in starts], axis=0
+    )
+    for back in order:
+        wait_leaf(fine_here, back, fine_sems)
+    asked = jnp.concatenate(asked, axis=0)
+    normal = mortar(part(fine_here), part(coarse_send), asked[:, QUAD : QUAD + 1], tangent_k)
+    write_partials(partial_out, partial_sums(normal, asked, back_k, elements), elements)
+
+    for back in order:
+        wait_leaf(coarse_here, back, coarse_sems)
+    normal = mortar(
+        fine, coarse_here[...].reshape(slots, 128), carried[:, QUAD : QUAD + 1], tangent_k
+    )
+    returned = face_rows(normal, position)
     for c in range(3):
         normals_out[c] = returned[c * 25 : c * 25 + 25]
-    wait_rows(fine_send, ranks - 1, send_sems.at[0])
-    wait_rows(normal_send, ranks - 1, send_sems.at[1])
+    for at, ref in enumerate((ask_send, fine_send, coarse_send)):
+        wait_rows(ref, ranks - 1, send_sems.at[at])
 
 
 def shards(parents, coarse, parent, octant, elem, side, owner, c_elem, c_side, quad):
@@ -510,6 +543,7 @@
     )
     args = [pltpu.with_memory_space_constraint(given[name], pltpu.HBM) for name in INPUTS]
     buffer = pltpu.VMEM((ranks, 2, 128), F32)
+    request = pltpu.VMEM((ranks, 1, 128), F32)
     far_first = sorted(range(leaves), key=lambda step: -min(step, leaves - step))
     groups = [far_first[at : at + GROUP] for at in range(0, leaves, GROUP)]
     shapes = (
@@ -526,12 +560,13 @@
             pltpu.VMEM((3 * POOL, 128), F32),
             pltpu.VMEM((8, 128), F32),
             pltpu.VMEM((8, 128), F32),
-            pltpu.VMEM((128, records), F32),
+            pltpu.VMEM((128, 2 * records), F32),
             pltpu.VMEM((384, coarse.shape[2]), F32),
-            buffer, buffer, buffer, buffer,
+            request, request, buffer, buffer, buffer, buffer,
             pltpu.SemaphoreType.DMA((len(args),)),
             pltpu.SemaphoreType.DMA((2,)),
-            pltpu.SemaphoreType.DMA((2,)),
+            pltpu.SemaphoreType.DMA((3,)),
+            pltpu.SemaphoreType.DMA((leaves,)),
             pltpu.SemaphoreType.DMA((leaves,)),
             pltpu.SemaphoreType.DMA((leaves,)),
         ],

time: 40.8 us -> 36.8 us (0.902)
  Pallas kernels: 38 us -> 34.1 us
    pallas_call x1, Pallas kernels: 38 us -> 34.1 us  [shards(): pl.pallas_call(functools.partial(kernel, leaves, doms, groups), out_shape...]
where the time goes in v5:
time: 36.8 us
  Pallas kernels  34.1 us (93%)
  local copies, waits for them, and re-layouts  2.07 us (6%)
  between operations  0.64 us (2%)
    pallas_call x1, Pallas kernels, shards(): pl.pallas_call(functools.partial(kernel, leaves, doms, groups), out_shape...  34.1 us
    unnamed x3, local copies, waits for them, and re-layouts  2.07 us

profile of v5, /device:TPU:1, one launch (start us, length us, event | category | flops | bytes accessed | tf_op | source)
XLA Modules:
  0.0 36.8 jit_solution(3447664658776243694)
XLA Ops:
  0.6 34.1 %shard_map.166 = (f32[125,256]{1,0:T(8,128)S(1)}, f32[3,25,256]{2,1,0:T(8,128)S(1)}, f32[3,150,256]{2,1,0:T(8,128)S(1)}) custom-call(s32[1,256]{1,0:T(1,128)} %bitcast.10, s32[1,256]{1,0:T(1,128)} %bitcast.11, s32[1,256]{1,0:T(1,128)} %bitcast.12, s32[1,256]{1,0:T(1,128)} %bitcast.13, s32[1,256]{1,0:T(1,128)} %bitcast.14, s32[1,256]{1,0:T(1,128)} %bitcast.15, ...), custom_call_target="tpu_custom_call" | custom-call | tf_op jit(solution)/shard_map/pallas_call | solution.py:554
  34.7 0.7 %copy.21 = f32[125,256]{1,0:T(8,128)} copy(f32[125,256]{1,0:T(8,128)S(1)} %get-tuple-element.6) | data formatting | bytes 256000
  35.4 0.6 %copy.22 = f32[3,25,256]{2,1,0:T(8,128)} copy(f32[3,25,256]{2,1,0:T(8,128)S(1)} %get-tuple-element.7) | data formatting | bytes 153600
  36.0 0.8 %copy.23 = f32[3,150,256]{2,1,0:T(8,128)} copy(f32[3,150,256]{2,1,0:T(8,128)S(1)} %get-tuple-element.8) | data formatting | bytes 921600

commit v6 on v5

--- a/solution.py
+++ b/solution.py
@@ -189,7 +189,8 @@
     records = owner.shape[1]
     column = columns_of(owner)[:, 0:1]
     same = (column == owner) & (iota((records, records), 0) < iota((records, records), 1))
-    return owner * 2.0 + jnp.sum(jnp.where(same, 1.0, 0.0), axis=0, keepdims=True)
+    rank = jnp.sum(jnp.where(same, 1.0, 0.0), axis=0, keepdims=True)
+    return owner * 2.0 + rank, column * 2.0 + columns_of(rank)[:, 0:1]
 
 
 def columns_of(rows):
@@ -314,11 +315,11 @@
     return both[:128] + both[128:]
 
 
-def face_rows(returned, position):
-    hot = ones_where(iota((returned.shape[0], position.shape[1]), 0) == position)
-    high, low = split(returned.T)
-    both = dot(jnp.concatenate([high, low], axis=0), hot)
-    return both[:128] + both[128:]
+def by_record(slot_rows, places):
+    high, low = split(slot_rows)
+    hot = ones_where(places == iota((places.shape[0], slot_rows.shape[0]), 1))
+    both = dot(hot, jnp.concatenate([high, low], axis=1))
+    return both[:, :128] + both[:, 128:]
 
 
 def fill_pool(pool, last, parents):
@@ -447,7 +448,7 @@
 
     names = ("parent", "octant", "elem", "side", "c_elem", "c_side", "quad")
     ints, keys = record_integers(*[load(name)[...].astype(F32) for name in names])
-    position = positions(load("owner")[...].astype(F32))
+    position, places = positions(load("owner")[...].astype(F32))
     ask_send[...] = requests(ints, ranks, position, wide).reshape(ask_send.shape)
     carried = slot_integers(ints, slots, position)
     fill_pool(pool, last, load("parents"))
@@ -455,6 +456,11 @@
     table = child_table(pool[...], child_k)
     sides = side_matrix(load("side_k")[...])
     fine, fine_keys = messages(table, sides, carried)
+
+    coarse = load("coarse")
+    elements = coarse.shape[2]
+    fill_coarse(scratch, coarse)
+    faces = coarse_faces(scratch[...], sides)
 
     pl.semaphore_wait(barrier, ranks - 1)
     after = lax.rem(me + 1, ranks)
@@ -478,10 +484,6 @@
         send_all(ahead, fine_send, fine_here, send_sems.at[1], fine_sems.at[ahead])
     fine_here[pl.ds(me, 1)] = fine_send[pl.ds(me, 1)]
 
-    coarse = load("coarse")
-    elements = coarse.shape[2]
-    fill_coarse(scratch, coarse)
-    faces = coarse_faces(scratch[...], sides)
     tangent_k = load("tangent_k")[...]
     back_k = load("back_k")[...]
     slope_k = load("slope_k")[...]
@@ -516,16 +518,27 @@
     normal = mortar(part(fine_here), part(coarse_send), asked[:, QUAD : QUAD + 1], tangent_k)
     write_partials(partial_out, partial_sums(normal, asked, back_k, elements), elements)
 
+    fine = by_record(fine, places)
+    quad = columns_of(ints)[:, QUAD : QUAD + 1]
     for back in order:
         wait_leaf(coarse_here, back, coarse_sems)
-    normal = mortar(
-        fine, coarse_here[...].reshape(slots, 128), carried[:, QUAD : QUAD + 1], tangent_k
-    )
-    returned = face_rows(normal, position)
+    coarse = by_record(coarse_here[...].reshape(slots, 128), places)
+    turned = mortar(fine, coarse, quad, tangent_k).T
     for c in range(3):
-        normals_out[c] = returned[c * 25 : c * 25 + 25]
+        normals_out[c] = turned[c * 25 : c * 25 + 25]
     for at, ref in enumerate((ask_send, fine_send, coarse_send)):
         wait_rows(ref, ranks - 1, send_sems.at[at])
+
+
+def store_kernel(*refs):
+    count = (len(refs) - 1) // 2
+    copies = [
+        pltpu.make_async_copy(refs[at], refs[count + at], refs[-1].at[at]) for at in range(count)
+    ]
+    for copy in copies:
+        copy.start()
+    for copy in copies:
+        copy.wait()
 
 
 def shards(parents, coarse, parent, octant, elem, side, owner, c_elem, c_side, quad):
@@ -551,7 +564,7 @@
         jax.ShapeDtypeStruct((3, 25, records), F32),
         jax.ShapeDtypeStruct((3, 150, coarse.shape[2]), F32),
     )
-    return pl.pallas_call(
+    results = pl.pallas_call(
         functools.partial(kernel, leaves, doms, groups),
         out_shape=shapes,
         in_specs=[pl.BlockSpec(memory_space=pltpu.HBM)] * len(args),
@@ -574,6 +587,14 @@
             collective_id=0, has_side_effects=True, vmem_limit_bytes=40 << 20
         ),
     )(*args)
+    return pl.pallas_call(
+        store_kernel,
+        out_shape=shapes,
+        in_specs=[pl.BlockSpec(memory_space=pl.ANY)] * 3,
+        out_specs=[pl.BlockSpec(memory_space=pltpu.HBM)] * 3,
+        scratch_shapes=[pltpu.SemaphoreType.DMA((3,))],
+        compiler_params=pltpu.CompilerParams(vmem_limit_bytes=4 << 20),
+    )(*results)
 
 
 def solution(mesh):

time: 36.8 us -> 35.1 us (0.954)
  local copies, waits for them, and re-layouts: 2.07 us -> 0 us
    unnamed x3 -> x0, local copies, waits for them, and re-layouts: 2.07 us -> none
    pallas_call x0 -> x1, Pallas kernels: none -> 0.87 us  [shards(): pl.pallas_call(store_kernel, out_shape=shapes, in_specs=[pl.BlockSpec(mem...]
    pallas_call x1, Pallas kernels: 34.1 us -> 33.5 us  [shards(): pl.pallas_call(functools.partial(kernel, leaves, doms, groups), out_shape...]
where the time goes in v6:
time: 35.1 us; the launch traced here: 35 us
  Pallas kernels  34.4 us (98%)
  between operations  0.64 us (2%)
    pallas_call x1, Pallas kernels, shards(): pl.pallas_call(functools.partial(kernel, leaves, doms, groups), out_shape...  33.5 us
    pallas_call x1, Pallas kernels, shards(): pl.pallas_call(store_kernel, out_shape=shapes, in_specs=[pl.BlockSpec(mem...  0.87 us

profile of v6, /device:TPU:1, one launch (start us, length us, event | category | flops | bytes accessed | tf_op | source)
XLA Modules:
  0.0 35.0 jit_solution(9934018550474514062)
XLA Ops:
  0.6 33.5 %shard_map.166 = (f32[125,256]{1,0:T(8,128)S(1)}, f32[3,25,256]{2,1,0:T(8,128)S(1)}, f32[3,150,256]{2,1,0:T(8,128)S(1)}) custom-call(s32[1,256]{1,0:T(1,128)} %bitcast.10, s32[1,256]{1,0:T(1,128)} %bitcast.11, s32[1,256]{1,0:T(1,128)} %bitcast.12, s32[1,256]{1,0:T(1,128)} %bitcast.13, s32[1,256]{1,0:T(1,128)} %bitcast.14, s32[1,256]{1,0:T(1,128)} %bitcast.15, ...), custom_call_target="tpu_custom_call" | custom-call | tf_op jit(solution)/shard_map/pallas_call | solution.py:567
  34.2 0.9 %shard_map.167 = (f32[125,256]{1,0:T(8,128)}, f32[3,25,256]{2,1,0:T(8,128)}, f32[3,150,256]{2,1,0:T(8,128)}) custom-call(f32[125,256]{1,0:T(8,128)S(1)} %get-tuple-element.6.refs_0_, f32[3,25,256]{2,1,0:T(8,128)S(1)} %get-tuple-element.7.refs_1_, f32[3,150,256]{2,1,0:T(8,128)S(1)} %get-tuple-element.8.refs_2_), custom_call_target="tpu_custom_call" | custom-call | tf_op jit(solution)/shard_map/pallas_call | solution.py:590

commit v7 on v6

--- a/solution.py
+++ b/solution.py
@@ -214,6 +214,9 @@
 
 
 def row_picker(key, size):
+    if size % 128 == 0:
+        hot = ones_where(key == iota((key.shape[0], size), 1))
+        return jnp.concatenate([hot, hot], axis=1)
     places = iota((key.shape[0], 2 * size), 1)
     places = jnp.where(places >= float(size), places - float(size), places)
     return ones_where(key == places)
@@ -243,10 +246,9 @@
 def expanded(rows):
     pairs = rows.shape[0]
     slot, pair = iota((2 * pairs, pairs), 0), iota((2 * pairs, pairs), 1)
-    first, second = ones_where(slot == 2.0 * pair), ones_where(slot == 2.0 * pair + 1.0)
-    rows = rows.astype(BF16)
-    both = dot(first, rows), pltpu.roll(dot(second, rows), SECOND, 1)
-    return both[0] + both[1]
+    hot = [ones_where(slot == 2.0 * pair), ones_where(slot == 2.0 * pair + 1.0)]
+    both = jnp.concatenate([rows, pltpu.roll(rows, SECOND, 1)], axis=0).astype(BF16)
+    return dot(jnp.concatenate(hot, axis=1), both)
 
 
 def messages(table, sides, carried):
@@ -277,16 +279,14 @@
 
 def coarse_faces(coarse, side_k):
     high, low = split(coarse.T)
-    return jnp.concatenate([dot(high, side_k), dot(low, side_k)], axis=1).astype(BF16)
+    return dot(jnp.concatenate([high, low], axis=0), side_k).astype(BF16)
 
 
 def coarse_rows(integers, faces):
     filled = integers[:, VALID : VALID + 1] > 0.5
     elem = jnp.where(filled, integers[:, ELEM : ELEM + 1], -1.0)
-    side = integers[:, SIDE : SIDE + 1]
-    hot = ones_where(elem == iota((integers.shape[0], faces.shape[0]), 1))
-    blocks = lane_blocks(dot(hot, faces), 12)
-    return pick(blocks[:6], side) + pick(blocks[6:], side)
+    hot = row_picker(elem, faces.shape[0] // 2)
+    return pick(lane_blocks(dot(hot, faces), 6), integers[:, SIDE : SIDE + 1])
 
 
 def mortar(fine, coarse, quad, tangent_k):
@@ -450,12 +450,10 @@
     ints, keys = record_integers(*[load(name)[...].astype(F32) for name in names])
     position, places = positions(load("owner")[...].astype(F32))
     ask_send[...] = requests(ints, ranks, position, wide).reshape(ask_send.shape)
-    carried = slot_integers(ints, slots, position)
     fill_pool(pool, last, load("parents"))
     child_k = load("child_k")[...]
     table = child_table(pool[...], child_k)
     sides = side_matrix(load("side_k")[...])
-    fine, fine_keys = messages(table, sides, carried)
 
     coarse = load("coarse")
     elements = coarse.shape[2]
@@ -476,6 +474,8 @@
     for ahead in far_first:
         send_all(ahead, ask_send, ask_here, send_sems.at[0], ask_sems.at[ahead])
     ask_here[pl.ds(me, 1)] = ask_send[pl.ds(me, 1)]
+    carried = slot_integers(ints, slots, position)
+    fine, fine_keys = messages(table, sides, carried)
     halo.wait()
     halo_table = child_table(jnp.concatenate([halo_in[c : c + 1] for c in range(3)], axis=0), child_k)
     fine = fine + halo_messages(halo_table, sides, fine_keys)

time: 35.1 us -> 35.1 us (level)
  no operation moved by 1% of the time
where the time goes in v7:
time: 35.1 us; the launch traced here: 35 us
  Pallas kernels  34.4 us (98%)
  between operations  0.64 us (2%)
    pallas_call x1, Pallas kernels, shards(): pl.pallas_call(functools.partial(kernel, leaves, doms, groups), out_shape...  33.5 us
    pallas_call x1, Pallas kernels, shards(): pl.pallas_call(store_kernel, out_shape=shapes, in_specs=[pl.BlockSpec(mem...  0.87 us

profile of v7, /device:TPU:1, one launch (start us, length us, event | category | flops | bytes accessed | tf_op | source)
XLA Modules:
  0.0 35.0 jit_solution(6010983887402765900)
XLA Ops:
  0.6 33.5 %shard_map.166 = (f32[125,256]{1,0:T(8,128)S(1)}, f32[3,25,256]{2,1,0:T(8,128)S(1)}, f32[3,150,256]{2,1,0:T(8,128)S(1)}) custom-call(s32[1,256]{1,0:T(1,128)} %bitcast.10, s32[1,256]{1,0:T(1,128)} %bitcast.11, s32[1,256]{1,0:T(1,128)} %bitcast.12, s32[1,256]{1,0:T(1,128)} %bitcast.13, s32[1,256]{1,0:T(1,128)} %bitcast.14, s32[1,256]{1,0:T(1,128)} %bitcast.15, ...), custom_call_target="tpu_custom_call" | custom-call | tf_op jit(solution)/shard_map/pallas_call | solution.py:567
  34.2 0.9 %shard_map.167 = (f32[125,256]{1,0:T(8,128)}, f32[3,25,256]{2,1,0:T(8,128)}, f32[3,150,256]{2,1,0:T(8,128)}) custom-call(f32[125,256]{1,0:T(8,128)S(1)} %get-tuple-element.6.refs_0_, f32[3,25,256]{2,1,0:T(8,128)S(1)} %get-tuple-element.7.refs_1_, f32[3,150,256]{2,1,0:T(8,128)S(1)} %get-tuple-element.8.refs_2_), custom_call_target="tpu_custom_call" | custom-call | tf_op jit(solution)/shard_map/pallas_call | solution.py:590
